TPU v7x, 128 devices: a whole 4x4x4 slice. The times are simulated.
128 devices in a mesh: kpair: 4 (over x_hi, core), band: 2 (over x_lo), pencil: 16 (over z, y).
Axes of the slice: x: 4 (x_hi: 2, x_lo: 2; x = x_hi * 2 + x_lo), y: 4, z: 4, core: 2. Of those that a mesh axis runs over, the one named last changes fastest.
Arguments:
- orbitals: float32 [2, 4, 2, 96, 9216], P(None, 'kpair', 'band', 'pencil'), may hold values from -6 to 6
- kcoords: int32 [4, 3], replicated, may hold values from 0 to 3, as said below
Outputs:
- exchange_vectors: float32 [2, 4, 2, 96, 9216], P(None, 'kpair', 'band', 'pencil')
Inputs may be any that keep to these rules, and one draw needn't show every extreme that they name: `kcoords`: each row is a point of a 4 x 4 x 4 k-point grid given by three integer coordinates; the rows are distinct.
All inputs are finite; a program needn't handle non-finite values.
Results may differ from a plain program's by a relative error of at most 0.0001.
Values sent between devices are 32-bit elements; how exact they have to be, the bound alone decides.
No kernel may reach another device: no remote copies, remote signals or barrier semaphores. Data moves between devices by JAX's collectives and lax.ppermute only.
A program may use at most 128 MiB of HBM per device.

v0:
```python
import math

import jax
import jax.numpy as jnp
import numpy as np
from jax import lax
from jax.experimental import pallas as pl
from jax.experimental.pallas import tpu as pltpu
from jax.sharding import PartitionSpec as P

GRID = 96
NB = 2
KPTS = 4
SCREENING = 0.5
RADIUS = GRID // 2 - 1
PENCILS = 16
SLAB = GRID // PENCILS
LANES = 128
ROWS = SLAB * GRID * GRID // LANES
CHUNK = 24

f32 = jnp.float32
bf16 = jnp.bfloat16

KZ = np.array([0] + [s * i for i in range(1, 48) for s in (1, -1)])
KY = np.array([[(8 * j + d // 2) * (1 - 2 * (d % 2)) for d in range(16)] for j in range(6)])
KY[0, 1] = -48
WIDTH = [
    2 * min(RADIUS, int(0.75 + math.sqrt(RADIUS**2 - max(0.0, 8 * j - 0.75) ** 2))) + 1
    for j in range(6)
]
SPLIT4 = LANES - WIDTH[3]
SPLIT5 = LANES - WIDTH[1]
FILL = {
    3: (4, 0, SPLIT4),
    0: (4, SPLIT4, WIDTH[4] - SPLIT4),
    1: (5, 0, SPLIT5),
    2: (5, SPLIT5, WIDTH[5] - SPLIT5),
}
for tile, (band, first, count) in FILL.items():
    assert WIDTH[tile] + count <= LANES


def split(values):
    high = jnp.asarray(values, f32).astype(bf16)
    low = (jnp.asarray(values, f32) - high.astype(f32)).astype(bf16)
    return high, low


def halves(table):
    table = np.asarray(table, np.float32)
    high = table.astype(bf16)
    low = (table - high.astype(np.float32)).astype(bf16)
    return np.stack([high, low])


def angles(rows, cols):
    product = np.outer(rows, cols) % GRID
    angle = product * (2.0 * math.pi / GRID)
    return np.cos(angle), np.sin(angle)


def build_tables():
    cosine, sine = angles(np.arange(GRID), KZ)
    forward_z = np.zeros((2, LANES, 2, LANES))
    inverse_z = np.zeros((2, LANES, 2, LANES))
    n = len(KZ)
    forward_z[0, :GRID, 0, :n] = cosine
    forward_z[1, :GRID, 0, :n] = sine
    forward_z[0, :GRID, 1, :n] = -sine
    forward_z[1, :GRID, 1, :n] = cosine
    inverse_z[0, :n, 0, :GRID] = cosine.T
    inverse_z[1, :n, 0, :GRID] = -sine.T
    inverse_z[0, :n, 1, :GRID] = sine.T
    inverse_z[1, :n, 1, :GRID] = cosine.T
    order_y = np.array([4 * g + j for j in range(4) for g in range(24)])
    cosine, sine = angles(KY.reshape(-1), order_y)
    forward_y = np.block([[cosine, sine], [-sine, cosine]])
    inverse_y = np.block([[cosine.T, -sine.T], [sine.T, cosine.T]])
    freq = np.where(np.arange(GRID) < GRID // 2, np.arange(GRID), np.arange(GRID) - GRID)
    cosine, sine = angles(freq, np.arange(GRID))
    full_f = np.block([[cosine, sine], [-sine, cosine]])
    full_i = np.block([[cosine.T, -sine.T], [sine.T, cosine.T]])
    forward_x = np.zeros((2, 2 * GRID, PENCILS, 16))
    inverse_x = np.zeros((2, PENCILS, 16, 2 * GRID))
    for h in range(2):
        for s in range(PENCILS):
            for c in range(2):
                rows = slice(4 * h + c * SLAB, 4 * h + (c + 1) * SLAB)
                xs = slice(c * GRID + s * SLAB, c * GRID + (s + 1) * SLAB)
                forward_x[h, :, s, rows] = full_f[:, xs]
                inverse_x[h, s, rows, :] = full_i[xs, :]
    lanes = np.zeros((8, 4 * LANES), np.float32)
    lanes[1] = 1000.0
    for tile in range(4):
        base = tile * LANES
        lanes[0, base : base + WIDTH[tile]] = tile
        lanes[1, base : base + WIDTH[tile]] = KZ[: WIDTH[tile]]
        band, first, count = FILL[tile]
        base += WIDTH[tile]
        lanes[0, base : base + count] = band
        lanes[1, base : base + count] = KZ[first : first + count]
    return dict(
        forward_z=halves(forward_z.reshape(2 * LANES, 2 * LANES)),
        inverse_z=halves(inverse_z.reshape(2 * LANES, 2 * LANES)),
        forward_y=halves(forward_y),
        inverse_y=halves(inverse_y),
        forward_x=halves(forward_x.reshape(2, 2 * GRID, 256)),
        inverse_x=halves(inverse_x.reshape(2, 256, 2 * GRID)),
        lanes=lanes,
    )


TABLES = build_tables()


def place():
    kpair = lax.axis_index("kpair")
    band = lax.axis_index("band")
    pencil = lax.axis_index("pencil")
    return kpair, band, pencil


def partners(kpair, band):
    core = kpair % 2
    chip = (kpair // 2) * 2 + band
    right_core = jnp.where(chip == 0, 1 - core, core)
    left_core = jnp.where(chip == 1, core, 1 - core)
    right = ((chip + 1) % 4 // 2) * 2 + right_core
    left = ((chip + 3) % 4 // 2) * 2 + left_core
    return right, left


def product3(left_high, left_low, right_high, right_low):
    dot = lambda a, b: jnp.dot(a, b, preferred_element_type=f32)
    return dot(left_high, right_high) + (dot(left_high, right_low) + dot(left_low, right_high))


def lane_index(rows):
    return lax.broadcasted_iota(jnp.int32, (rows, LANES), 1)


def chunk_row(tile, part, x):
    return (tile % 2) * CHUNK + (tile // 2) * 12 + part * SLAB + x


VMEM_LIMIT = 12 * 1024 * 1024


SPACE = {"vmem": pltpu.VMEM, "hbm": pltpu.HBM}


def kept_in(place, array):
    return pltpu.with_memory_space_constraint(array, SPACE[place]) if place in SPACE else array


class Fetched:
    def __init__(self, source, target, semaphore):
        self.target = target
        self.copy = pltpu.make_async_copy(source, target, semaphore)
        self.copy.start()
        self.pending = True

    def get(self):
        if self.pending:
            self.copy.wait()
            self.pending = False
        return self.target


class Ready:
    def __init__(self, ref):
        self.ref = ref

    def get(self):
        return self.ref


def call(kernel, out_shapes, scratch, args, interpret=False):
    places = [place for place, _ in args]
    arrays = [jnp.asarray(array) for _, array in args]
    specs = {
        "smem": pl.BlockSpec(memory_space=pltpu.SMEM),
        "vmem": pl.BlockSpec(memory_space=pltpu.VMEM),
        "hbm": pl.BlockSpec(memory_space=pltpu.HBM),
    }
    remote = [array for place, array in zip(places, arrays) if place == "hbm"]
    n_in, n_out = len(args), len(out_shapes)

    def entry(*refs):
        inputs, outputs = refs[:n_in], refs[n_in : n_in + n_out]
        rest = refs[n_in + n_out :]
        targets, semaphores, own_scratch = rest[: len(remote)], rest[len(remote)], rest[len(remote) + 1 :]
        handles, k = [], 0
        for place, ref in zip(places, inputs):
            if place == "hbm":
                handles.append(Fetched(ref, targets[k], semaphores.at[k]))
                k += 1
            else:
                handles.append(Ready(ref))
        kernel(*handles, *outputs, *own_scratch)

    return pl.pallas_call(
        entry,
        out_shape=out_shapes,
        in_specs=[specs[place] for place in places],
        out_specs=[specs["vmem"]] * n_out,
        scratch_shapes=[pltpu.VMEM(array.shape, array.dtype) for array in remote]
        + [pltpu.SemaphoreType.DMA((max(1, len(remote)),))]
        + scratch,
        interpret=interpret,
        compiler_params=pltpu.CompilerParams(vmem_limit_bytes=VMEM_LIMIT),
    )(*(kept_in(place, array) for place, array in zip(places, arrays)))


LOCAL = (("local", 0, 1),)
REMOTE = (("across", 1, 2), ("right", 0, 1), ("left", 0, 2))


def density_kernel(tasks, members, where, *refs):
    n = len(tasks)
    orbitals = refs[:members]
    z_table, y_table, out_ref, dens_ref, high_ref, low_ref = refs[members:]
    kpair, _, _ = where()
    lane = lane_index(24)
    lane16 = lane_index(16)
    for task, (kind, a, b) in enumerate(tasks):
        own_ref, far_ref = orbitals[a].get(), orbitals[b].get()
        own_real, own_imag = own_ref[0:ROWS, :], own_ref[ROWS : 2 * ROWS, :]
        far_real, far_imag = far_ref[0:ROWS, :], far_ref[ROWS : 2 * ROWS, :]
        real = far_real * own_real + far_imag * own_imag
        imag = far_real * own_imag - far_imag * own_real
        if kind == "local":
            packed = kpair % 2 == 1
            real = jnp.where(packed, own_real * own_real + own_imag * own_imag, real)
            imag = jnp.where(packed, far_real * far_real + far_imag * far_imag, imag)
        dens_ref[0:ROWS, :] = real
        dens_ref[ROWS : 2 * ROWS, :] = imag
        for c in range(2):
            cols = slice(c * LANES, (c + 1) * LANES)
            for x in range(SLAB):
                first = c * ROWS + x * 72
                t0, t1, t2 = (dens_ref[pl.ds(first + s, 24, stride=3), :] for s in range(3))
                rows = (
                    t0,
                    jnp.where(lane < 32, pltpu.roll(t0, 32, 1), pltpu.roll(t1, 32, 1)),
                    jnp.where(lane < 64, pltpu.roll(t1, 64, 1), pltpu.roll(t2, 64, 1)),
                    pltpu.roll(t2, 96, 1),
                )
                high, low = split(jnp.concatenate(rows, axis=0))
                high_ref[x * GRID : (x + 1) * GRID, cols] = high
                low_ref[x * GRID : (x + 1) * GRID, cols] = low
        z_ref = z_table.get()
        along_z = product3(high_ref[...], low_ref[...], z_ref[0], z_ref[1])
        high, low = split(along_z)
        high_ref[...] = high
        low_ref[...] = low
        y_ref = y_table.get()
        for x in range(0, SLAB, 2):
            def columns(ref):
                return jnp.concatenate(
                    [
                        jnp.concatenate(
                            [ref[v * GRID : (v + 1) * GRID, 0:LANES], ref[v * GRID : (v + 1) * GRID, LANES:]],
                            axis=0,
                        )
                        for v in (x, x + 1)
                    ],
                    axis=1,
                )

            along_y = product3(y_ref[0], y_ref[1], columns(high_ref), columns(low_ref))
            for v in range(2):
                for c in range(2):
                    bands = [
                        along_y[c * GRID + 16 * j : c * GRID + 16 * j + 16, v * LANES : (v + 1) * LANES]
                        for j in range(6)
                    ]
                    for tile in range(4):
                        band, start, _ = FILL[tile]
                        shift = (WIDTH[tile] - start) % LANES
                        value = jnp.where(lane16 < WIDTH[tile], bands[tile], pltpu.roll(bands[band], shift, 1))
                        row = task * 2 * CHUNK + chunk_row(tile, c, x + v)
                        out_ref[pl.ds(row, 16, stride=n * 2 * CHUNK), :] = value


def scratch_fields():
    return [
        pltpu.VMEM((2 * ROWS, LANES), f32),
        pltpu.VMEM((SLAB * GRID, 2 * LANES), bf16),
        pltpu.VMEM((SLAB * GRID, 2 * LANES), bf16),
    ]


def densities(tasks, orbitals, where=place, interpret=False):
    n = len(tasks)
    (out,) = call(
        lambda *refs: density_kernel(tasks, len(orbitals), where, *refs),
        [pltpu.HBM((PENCILS * n * 2 * CHUNK, LANES), f32)],
        scratch_fields(),
        [*orbitals, ("hbm", TABLES["forward_z"]), ("hbm", TABLES["forward_y"])],
        interpret,
    )
    return out.reshape(PENCILS, n, 2, CHUNK, LANES)


def filter_kernel(tasks, where, coords, chunks, lanes, forward_table, inverse_table, out_ref):
    coords_ref, in_ref, lanes_ref = coords.get(), chunks.get(), lanes.get()
    kpair, band, pencil = where()
    right, left = partners(kpair, band)
    points = {
        "local": (kpair, jnp.where(kpair % 2 == 1, kpair, kpair + 1)),
        "right": (kpair, right),
        "left": (kpair, left),
        "across": (right, left),
    }
    factor = (2.0 * math.pi / GRID) ** 2
    scale = -1.0 / (KPTS * NB) / GRID**3
    slot = lanes_ref[0:1, :]
    sign = (1 - 2 * (pencil % 2)).astype(f32)
    ky = sign * (8.0 * slot + (pencil // 2).astype(f32))
    ky = jnp.where(slot == jnp.where(pencil == 1, 0.0, -1.0), -48.0, ky)
    kz = lanes_ref[1:2, :]
    index = lax.broadcasted_iota(jnp.int32, (GRID, 2 * LANES), 0)
    kx = jnp.where(index < GRID // 2, index, index - GRID).astype(f32)
    for task, (kind, _, _) in enumerate(tasks):
        here, there = points[kind]
        shift = [(coords_ref[here, a] - coords_ref[there, a]).astype(f32) * 0.25 for a in range(3)]
        plane = (ky + shift[1]) ** 2 + (kz + shift[2]) ** 2
        along_x = (kx + shift[0]) ** 2
        previous = None
        for h in range(2):
            rows = [
                in_ref[:, task, l, 8 * h : 8 * h + 16, :].reshape(256, LANES) for l in range(2)
            ]
            high, low = split(jnp.concatenate(rows, axis=1))
            forward_ref = forward_table.get()
            spectrum = product3(forward_ref[0, h], forward_ref[1, h], high, low)
            squared = along_x + plane[:, h * 256 : (h + 1) * 256]
            coulomb = jnp.where(
                squared <= RADIUS * RADIUS, 4.0 * math.pi / (factor * squared + SCREENING), 0.0
            ) * scale
            spectrum = jnp.concatenate([spectrum[:GRID] * coulomb, spectrum[GRID:] * coulomb], axis=0)
            high, low = split(spectrum)
            inverse_ref = inverse_table.get()
            back = product3(inverse_ref[0, h], inverse_ref[1, h], high, low).reshape(PENCILS, 16, 2 * LANES)
            for l in range(2):
                part = back[:, :, l * LANES : (l + 1) * LANES]
                if h == 0:
                    out_ref[:, task, l, 0:8, :] = part[:, 0:8]
                else:
                    out_ref[:, task, l, 16:24, :] = part[:, 8:16]
                    out_ref[:, task, l, 8:16, :] = part[:, 0:8] + previous[:, 8:16, l * LANES : (l + 1) * LANES]
            previous = back


def filtered(tasks, coords, chunks, source, where=place, interpret=False):
    (out,) = call(
        lambda *refs: filter_kernel(tasks, where, *refs),
        [pltpu.HBM(chunks.shape, f32)],
        [],
        [
            ("smem", coords),
            (source, chunks),
            ("hbm", TABLES["lanes"]),
            ("hbm", TABLES["forward_x"]),
            ("hbm", TABLES["inverse_x"]),
        ],
        interpret,
    )
    return out


def potential_kernel(tasks, members, where, chunks, *refs):
    n = len(tasks)
    in_ref = chunks.get()
    orbitals = refs[:members]
    y_table, z_table = refs[members : members + 2]
    sum_refs = refs[members + 2 : 2 * members + 2]
    pot_ref, high_ref, low_ref = refs[2 * members + 2 :]
    touched = set()
    kpair, _, _ = where()
    lane = lane_index(24)
    lane16 = lane_index(16)
    for task, (kind, a, b) in enumerate(tasks):
        for x in range(0, SLAB, 2):
            pair = []
            for v in (x, x + 1):
                parts = []
                for c in range(2):
                    tiles = [
                        in_ref[pl.ds(task * 2 * CHUNK + chunk_row(t, c, v), 16, stride=n * 2 * CHUNK), :]
                        for t in range(4)
                    ]
                    bands = [jnp.where(lane16 < WIDTH[t], tiles[t], 0.0) for t in range(4)]
                    for (ta, tb) in ((3, 0), (1, 2)):
                        _, sa, ca = FILL[ta]
                        _, sb, cb = FILL[tb]
                        head = pltpu.roll(tiles[ta], (sa - WIDTH[ta]) % LANES, 1)
                        tail = pltpu.roll(tiles[tb], (sb - WIDTH[tb]) % LANES, 1)
                        bands.append(jnp.where(lane16 < ca, head, jnp.where(lane16 < ca + cb, tail, 0.0)))
                    parts += bands
                pair.append(jnp.concatenate(parts, axis=0))
            high, low = split(jnp.concatenate(pair, axis=1))
            y_ref = y_table.get()
            along_y = product3(y_ref[0], y_ref[1], high, low)
            high, low = split(along_y)
            for v in range(2):
                for c in range(2):
                    rows = slice((x + v) * GRID, (x + v + 1) * GRID)
                    cols = slice(c * LANES, (c + 1) * LANES)
                    high_ref[rows, cols] = high[c * GRID : (c + 1) * GRID, v * LANES : (v + 1) * LANES]
                    low_ref[rows, cols] = low[c * GRID : (c + 1) * GRID, v * LANES : (v + 1) * LANES]
        z_ref = z_table.get()
        along_z = product3(high_ref[...], low_ref[...], z_ref[0], z_ref[1])
        for c in range(2):
            for x in range(SLAB):
                v0, v1, v2, v3 = (
                    along_z[x * GRID + 24 * j : x * GRID + 24 * j + 24, c * LANES : (c + 1) * LANES]
                    for j in range(4)
                )
                v1, v2, v3 = pltpu.roll(v1, 96, 1), pltpu.roll(v2, 64, 1), pltpu.roll(v3, 32, 1)
                rows = (jnp.where(lane < 96, v0, v1), jnp.where(lane < 64, v1, v2), jnp.where(lane < 32, v2, v3))
                for s in range(3):
                    pot_ref[pl.ds(c * ROWS + x * 72 + s, 24, stride=3), :] = rows[s]
        own_ref, far_ref = orbitals[a].get(), orbitals[b].get()
        own_real, own_imag = own_ref[0:ROWS, :], own_ref[ROWS : 2 * ROWS, :]
        far_real, far_imag = far_ref[0:ROWS, :], far_ref[ROWS : 2 * ROWS, :]
        pot_real, pot_imag = pot_ref[0:ROWS, :], pot_ref[ROWS : 2 * ROWS, :]
        here_real = far_real * pot_real - far_imag * pot_imag
        here_imag = far_real * pot_imag + far_imag * pot_real
        there_real = own_real * pot_real + own_imag * pot_imag
        there_imag = own_imag * pot_real - own_real * pot_imag
        if kind == "local":
            packed = kpair % 2 == 1
            here_real = jnp.where(packed, own_real * pot_real, here_real)
            here_imag = jnp.where(packed, own_imag * pot_real, here_imag)
            there_real = jnp.where(packed, far_real * pot_imag, there_real)
            there_imag = jnp.where(packed, far_imag * pot_imag, there_imag)
        for member, real, imag in ((a, here_real, here_imag), (b, there_real, there_imag)):
            if member in touched:
                real = real + sum_refs[member][0:ROWS, :]
                imag = imag + sum_refs[member][ROWS : 2 * ROWS, :]
            touched.add(member)
            sum_refs[member][0:ROWS, :] = real
            sum_refs[member][ROWS : 2 * ROWS, :] = imag


def potentials(tasks, chunks, orbitals, where=place, interpret=False):
    n = len(tasks)
    return call(
        lambda *refs: potential_kernel(tasks, len(orbitals), where, *refs),
        [pltpu.HBM((2 * ROWS, LANES), f32)] * len(orbitals),
        scratch_fields(),
        [
            ("vmem", chunks.reshape(PENCILS * n * 2 * CHUNK, LANES)),
            *orbitals,
            ("hbm", TABLES["inverse_y"]),
            ("hbm", TABLES["inverse_z"]),
        ],
        interpret,
    )


def line(chip, core):
    chip %= 4
    return (chip // 2) * 4 + core * 2 + chip % 2


TURN = (1, 0, 0, 0)


def route(kind):
    pairs = []
    for chip in range(4):
        for core in range(2):
            if kind == "local":
                source = line(chip, 1 - core)
            elif kind == "right":
                source = line(chip + 1, core ^ TURN[chip])
            else:
                source = line(chip - 1, core ^ (1 - TURN[chip - 1]))
            pairs.append((source, line(chip, core)))
    return pairs


def fetch(kind, block):
    return lax.ppermute(block, ("kpair", "band"), route(kind))


def give_back(kind, block):
    return lax.ppermute(block, ("kpair", "band"), [(b, a) for a, b in route(kind)])


def transpose(chunks):
    return lax.all_to_all(chunks, "pencil", 0, 0, tiled=True)


def body(orbitals, kcoords):
    own = orbitals.reshape(2 * ROWS, LANES)
    right, left, other = fetch("right", own), fetch("left", own), fetch("local", own)
    near = [("hbm", own), ("vmem", other)]
    far = [("hbm", own), ("vmem", right), ("vmem", left)]
    chunks_near = densities(LOCAL, near)
    sent_near = transpose(chunks_near)
    chunks_far = densities(REMOTE, far)
    sent_far = transpose(chunks_far)
    spectrum_near = filtered(LOCAL, kcoords, sent_near, "hbm")
    spectrum_far = filtered(REMOTE, kcoords, sent_far, "vmem")
    back_far = transpose(spectrum_far)
    back_far, spectrum_near = lax.optimization_barrier((back_far, spectrum_near))
    back_near = transpose(spectrum_near)
    far_sum, for_right, for_left = potentials(REMOTE, back_far, far)
    from_right, from_left = give_back("right", for_right), give_back("left", for_left)
    near_sum, for_other = potentials(LOCAL, back_near, near)
    from_other = give_back("local", for_other)
    out = (far_sum + near_sum) + from_other + (from_right + from_left)
    return out.reshape(2, 1, 1, SLAB, GRID * GRID)


def solution(mesh):
    in_specs = (P(None, "kpair", "band", "pencil", None), P())
    out_specs = P(None, "kpair", "band", "pencil", None)
    return jax.shard_map(body, mesh=mesh, in_specs=in_specs, out_specs=out_specs, check_vma=False)
```

profile of v0, /device:TPU:0, one launch (start us, length us, event | category | flops | bytes accessed | tf_op | source)
XLA Modules:
  0.0 106.4 jit_solution(12681720329192557764)
XLA Ops:
  0.0 1.6 %collective-permute-start.1 = (f32[864,128]{1,0:T(8,128)}, f32[864,128]{1,0:T(8,128)S(1)}, u32[]{:S(2)}, u32[]{:S(2)}) collective-permute-start(f32[864,128]{1,0:T(8,128)} %bitcast.8), channel_id=1, source_target_pairs={{112,0},{80,32},{0,16},{32,48},{48,64},{16,96},{96,80},{64,112},{1... | collective-permute-start | bytes 1327112 | tf_op jit(solution)/shard_map/ppermute | solution.py:488
  1.6 1.3 %collective-permute-start = (f32[864,128]{1,0:T(8,128)}, f32[864,128]{1,0:T(8,128)S(1)}, u32[]{:S(2)}, u32[]{:S(2)}) collective-permute-start(f32[864,128]{1,0:T(8,128)} %bitcast.9), channel_id=1, source_target_pairs={{48,0},{16,32},{64,16},{96,48},{80,64},{112,96},{0,80},{32,112},{4... | collective-permute-start | bytes 1327112 | tf_op jit(solution)/shard_map/ppermute | solution.py:488
  2.9 10.8 %collective-permute-done.1.refs_2_.refs_3_ = f32[864,128]{1,0:T(8,128)S(1)} collective-permute-done((f32[864,128]{1,0:T(8,128)}, f32[864,128]{1,0:T(8,128)S(1)}, u32[]{:S(2)}, u32[]{:S(2)}) %collective-permute-start.1) | collective-permute-done | bytes 442400 | tf_op jit(solution)/shard_map/ppermute | solution.py:488
  13.7 0.3 collective-permute-done.refs_1_.refs_2_
  14.0 5.5 %shard_map.91 = f32[2304,128]{1,0:T(8,128)} custom-call(f32[864,128]{1,0:T(8,128)} %bitcast.10, f32[864,128]{1,0:T(8,128)S(1)} %collective-permute-done.refs_1_.refs_2_, f32[864,128]{1,0:T(8,128)S(1)} %collective-permute-done.1.refs_2_.refs_3_, bf16[2,256,256]{2,1,0:T(8,128)(2,1)} %constant.14.clone.refs_3_.refs_2_, ...), custom_call_target="tpu_custom_call" | custom-call | tf_op jit(solution)/shard_map/pallas_call | solution.py:203
  19.5 8.2 %all-to-all-start = ((f32[16,3,2,24,128]{4,3,2,1,0:T(8,128)}), f32[16,3,2,24,128]{4,3,2,1,0:T(8,128)S(1)}, u32[]{:S(2)}, u32[]{:S(2)}) async-start(f32[16,3,2,24,128]{4,3,2,1,0:T(8,128)} %bitcast.15), calls=%async_computation | async-start | bytes 2359296 | tf_op jit(solution)/shard_map/all_to_all | solution.py:496
  27.7 0.1 collective-permute-start.2
  27.8 1.8 %collective-permute-done.2.refs_1_.refs_2_ = f32[864,128]{1,0:T(8,128)S(1)} collective-permute-done((f32[864,128]{1,0:T(8,128)S(1)}, f32[864,128]{1,0:T(8,128)S(1)}, u32[]{:S(2)}, u32[]{:S(2)}) %collective-permute-start.2) | collective-permute-done | bytes 442400 | tf_op jit(solution)/shard_map/ppermute | solution.py:488
  29.6 3.4 %shard_map.93 = f32[768,128]{1,0:T(8,128)} custom-call(f32[864,128]{1,0:T(8,128)} %bitcast.11, f32[864,128]{1,0:T(8,128)S(1)} %collective-permute-done.2.refs_1_.refs_2_, bf16[2,256,256]{2,1,0:T(8,128)(2,1)} %constant.14.clone.refs_3_.refs_2_, bf16[2,192,192]{2,1,0:T(8,128)(2,1)} %constant.15.clone.refs_4_.refs_3_), custom_call_target="tpu_custom_call" | custom-call | tf_op jit(solution)/shard_map/pallas_call | solution.py:203
  33.0 14.1 %all-to-all-done.refs_1_ = f32[16,3,2,24,128]{4,3,2,1,0:T(8,128)S(1)} async-done(((f32[16,3,2,24,128]{4,3,2,1,0:T(8,128)}), f32[16,3,2,24,128]{4,3,2,1,0:T(8,128)S(1)}, u32[]{:S(2)}, u32[]{:S(2)}) %all-to-all-start) | async-done | bytes 1179680 | tf_op jit(solution)/shard_map/all_to_all | solution.py:496
  47.1 3.6 %all-to-all-start.2 = ((f32[16,1,2,24,128]{4,3,2,1,0:T(8,128)}), f32[16,1,2,24,128]{4,3,2,1,0:T(8,128)S(1)}, u32[]{:S(2)}, u32[]{:S(2)}) async-start(f32[16,1,2,24,128]{4,3,2,1,0:T(8,128)} %bitcast.16), calls=%async_computation.2 | async-start | bytes 786432 | tf_op jit(solution)/shard_map/all_to_all | solution.py:496
  50.7 4.6 %shard_map.92 = f32[16,3,2,24,128]{4,3,2,1,0:T(8,128)} custom-call(s32[4,3]{1,0:T(4,128)S(1)} %copy-done, f32[16,3,2,24,128]{4,3,2,1,0:T(8,128)S(1)} %all-to-all-done.refs_1_, f32[8,512]{1,0:T(8,128)} %constant.16.clone.refs_2_, bf16[2,2,192,256]{3,2,1,0:T(8,128)(2,1)} %constant.17.clone.refs_3_, bf16[2,2,256,192]{3,2,1,0:T(8,128)(2,1)} %constant.18.clone.refs_4_), custom_call_target="tpu_custom_call" | custom-call | tf_op jit(solution)/shard_map/pallas_call | solution.py:203
  55.3 5.3 %all-to-all-done.2.refs_1_ = f32[16,1,2,24,128]{4,3,2,1,0:T(8,128)S(1)} async-done(((f32[16,1,2,24,128]{4,3,2,1,0:T(8,128)}), f32[16,1,2,24,128]{4,3,2,1,0:T(8,128)S(1)}, u32[]{:S(2)}, u32[]{:S(2)}) %all-to-all-start.2) | async-done | bytes 393248 | tf_op jit(solution)/shard_map/all_to_all | solution.py:496
  60.6 3.7 %all-to-all-start.1 = ((f32[16,3,2,24,128]{4,3,2,1,0:T(8,128)}), f32[16,3,2,24,128]{4,3,2,1,0:T(8,128)S(1)}, u32[]{:S(2)}, u32[]{:S(2)}) async-start(f32[16,3,2,24,128]{4,3,2,1,0:T(8,128)} %shard_map.92), calls=%async_computation.1 | async-start | bytes 2359296 | tf_op jit(solution)/shard_map/all_to_all | solution.py:496
  64.3 3.4 %shard_map.94 = f32[16,1,2,24,128]{4,3,2,1,0:T(8,128)} custom-call(s32[4,3]{1,0:T(4,128)S(1)} %copy-done, f32[16,1,2,24,128]{4,3,2,1,0:T(8,128)} %copy-done.2, f32[8,512]{1,0:T(8,128)} %constant.16.clone.refs_2_, bf16[2,2,192,256]{3,2,1,0:T(8,128)(2,1)} %constant.17.clone.refs_3_, bf16[2,2,256,192]{3,2,1,0:T(8,128)(2,1)} %constant.18.clone.refs_4_), custom_call_target="tpu_custom_call" | custom-call | tf_op jit(solution)/shard_map/pallas_call | solution.py:203
  67.7 14.5 %all-to-all-done.1 = f32[16,3,2,24,128]{4,3,2,1,0:T(8,128)S(1)} async-done(((f32[16,3,2,24,128]{4,3,2,1,0:T(8,128)}), f32[16,3,2,24,128]{4,3,2,1,0:T(8,128)S(1)}, u32[]{:S(2)}, u32[]{:S(2)}) %all-to-all-start.1) | async-done | bytes 1179680 | tf_op jit(solution)/shard_map/all_to_all | solution.py:496
  82.3 3.6 %all-to-all-start.3 = ((f32[16,1,2,24,128]{4,3,2,1,0:T(8,128)}), f32[16,1,2,24,128]{4,3,2,1,0:T(8,128)S(1)}, u32[]{:S(2)}, u32[]{:S(2)}) async-start(f32[16,1,2,24,128]{4,3,2,1,0:T(8,128)} %shard_map.94), calls=%async_computation.3 | async-start | bytes 786432 | tf_op jit(solution)/shard_map/all_to_all | solution.py:496
  85.8 5.3 %shard_map.95 = (f32[864,128]{1,0:T(8,128)}, f32[864,128]{1,0:T(8,128)}, f32[864,128]{1,0:T(8,128)}) custom-call(f32[2304,128]{1,0:T(8,128)S(1)} %bitcast.6, f32[864,128]{1,0:T(8,128)} %bitcast.12, f32[864,128]{1,0:T(8,128)S(1)} %collective-permute-done.refs_1_.refs_2_, f32[864,128]{1,0:T(8,128)S(1)} %collective-permute-done.1.refs_2_.refs_3_, ...), custom_call_target="tpu_custom_call" | custom-call | tf_op jit(solution)/shard_map/pallas_call | solution.py:203
  91.3 1.1 %collective-permute-start.5 = (f32[864,128]{1,0:T(8,128)}, f32[864,128]{1,0:T(8,128)S(1)}, u32[]{:S(2)}, u32[]{:S(2)}) collective-permute-start(f32[864,128]{1,0:T(8,128)} %get-tuple-element.18), channel_id=1, source_target_pairs={{0,112},{32,80},{16,0},{48,32},{64,48},{96,16},{80,96},{112,64},{1... | collective-permute-start | bytes 1327112 | tf_op jit(solution)/shard_map/ppermute | solution.py:492
  92.4 2.8 %all-to-all-done.3 = f32[16,1,2,24,128]{4,3,2,1,0:T(8,128)S(1)} async-done(((f32[16,1,2,24,128]{4,3,2,1,0:T(8,128)}), f32[16,1,2,24,128]{4,3,2,1,0:T(8,128)S(1)}, u32[]{:S(2)}, u32[]{:S(2)}) %all-to-all-start.3) | async-done | bytes 393248 | tf_op jit(solution)/shard_map/all_to_all | solution.py:496
  95.2 3.2 %shard_map.96 = (f32[864,128]{1,0:T(8,128)}, f32[864,128]{1,0:T(8,128)}) custom-call(f32[768,128]{1,0:T(8,128)S(1)} %bitcast.7, f32[864,128]{1,0:T(8,128)} %bitcast.13, f32[864,128]{1,0:T(8,128)S(1)} %collective-permute-done.2.refs_1_.refs_2_, bf16[2,192,192]{2,1,0:T(8,128)(2,1)} %constant.19.clone.refs_4_.refs_3_, ...), custom_call_target="tpu_custom_call" | custom-call | tf_op jit(solution)/shard_map/pallas_call | solution.py:203
  98.5 4.8 %collective-permute-done.4 = f32[864,128]{1,0:T(8,128)S(1)} collective-permute-done((f32[864,128]{1,0:T(8,128)}, f32[864,128]{1,0:T(8,128)S(1)}, u32[]{:S(2)}, u32[]{:S(2)}) %collective-permute-start.4) | collective-permute-done | bytes 442400 | tf_op jit(solution)/shard_map/ppermute | solution.py:492
  103.3 1.3 %collective-permute-done.5 = f32[864,128]{1,0:T(8,128)S(1)} collective-permute-done((f32[864,128]{1,0:T(8,128)}, f32[864,128]{1,0:T(8,128)S(1)}, u32[]{:S(2)}, u32[]{:S(2)}) %collective-permute-start.5) | collective-permute-done | bytes 442400 | tf_op jit(solution)/shard_map/ppermute | solution.py:492
  104.6 1.9 %add_add_fusion = f32[864,128]{1,0:T(8,128)} fusion(f32[864,128]{1,0:T(8,128)S(1)} %collective-permute-done.4, f32[864,128]{1,0:T(8,128)S(1)} %collective-permute-done.5, f32[864,128]{1,0:T(8,128)S(1)} %collective-permute-done.3, f32[864,128]{1,0:T(8,128)S(1)} %copy-done.3, f32[864,128]{1,0:T(8,128)} %get-tuple-element.15), kind=kLoop, calls=%fused_computation | loop fusion | flops 442368 | bytes 2654208 | tf_op jit(solution)/shard_map/add | solution.py:517
  (11 shorter events, 0.2 us)
Async XLA Ops:
  0.0 13.7 %collective-permute-start.1 = (f32[864,128]{1,0:T(8,128)}, f32[864,128]{1,0:T(8,128)S(1)}, u32[]{:S(2)}, u32[]{:S(2)}) collective-permute-start(f32[864,128]{1,0:T(8,128)} %bitcast.8), channel_id=1, source_target_pairs={{112,0},{80,32},{0,16},{32,48},{48,64},{16,96},{96,80},{64,112},{1... | collective-permute-start | bytes 1327112 | tf_op jit(solution)/shard_map/ppermute | solution.py:488
  1.6 12.4 %collective-permute-start = (f32[864,128]{1,0:T(8,128)}, f32[864,128]{1,0:T(8,128)S(1)}, u32[]{:S(2)}, u32[]{:S(2)}) collective-permute-start(f32[864,128]{1,0:T(8,128)} %bitcast.9), channel_id=1, source_target_pairs={{48,0},{16,32},{64,16},{96,48},{80,64},{112,96},{0,80},{32,112},{4... | collective-permute-start | bytes 1327112 | tf_op jit(solution)/shard_map/ppermute | solution.py:488
  19.5 8.2 %copy-start.1 = (f32[2,1,1,6,9216]{4,2,3,1,0:T(1,128)S(1)}, f32[2,1,1,6,9216]{4,2,3,1,0:T(1,128)}, u32[]{:S(2)}) copy-start(f32[2,1,1,6,9216]{4,2,3,1,0:T(1,128)} %param.9) | copy-start | bytes 1327108
  19.5 27.6 %all-to-all-start = ((f32[16,3,2,24,128]{4,3,2,1,0:T(8,128)}), f32[16,3,2,24,128]{4,3,2,1,0:T(8,128)S(1)}, u32[]{:S(2)}, u32[]{:S(2)}) async-start(f32[16,3,2,24,128]{4,3,2,1,0:T(8,128)} %bitcast.15), calls=%async_computation | async-start | bytes 2359296 | tf_op jit(solution)/shard_map/all_to_all | solution.py:496
  27.7 23.0 %copy-start = (s32[4,3]{1,0:T(4,128)S(1)}, s32[4,3]{1,0:T(4,128)}, u32[]{:S(2)}) copy-start(s32[4,3]{1,0:T(4,128)} %refs_0_.3) | copy-start | bytes 148
  27.7 1.9 %collective-permute-start.2 = (f32[864,128]{1,0:T(8,128)S(1)}, f32[864,128]{1,0:T(8,128)S(1)}, u32[]{:S(2)}, u32[]{:S(2)}) collective-permute-start(f32[864,128]{1,0:T(8,128)S(1)} %bitcast.14), channel_id=1, source_target_pairs={{32,0},{0,32},{48,16},{16,48},{96,64},{64,96},{112,80},{80,112},{3... | collective-permute-start | bytes 1327112 | tf_op jit(solution)/shard_map/ppermute | solution.py:488
  47.1 13.5 %all-to-all-start.2 = ((f32[16,1,2,24,128]{4,3,2,1,0:T(8,128)}), f32[16,1,2,24,128]{4,3,2,1,0:T(8,128)S(1)}, u32[]{:S(2)}, u32[]{:S(2)}) async-start(f32[16,1,2,24,128]{4,3,2,1,0:T(8,128)} %bitcast.16), calls=%async_computation.2 | async-start | bytes 786432 | tf_op jit(solution)/shard_map/all_to_all | solution.py:496
  60.6 3.7 %copy-start.2 = (f32[16,1,2,24,128]{4,3,2,1,0:T(8,128)}, f32[16,1,2,24,128]{4,3,2,1,0:T(8,128)S(1)}, u32[]{:S(2)}) copy-start(f32[16,1,2,24,128]{4,3,2,1,0:T(8,128)S(1)} %all-to-all-done.2.refs_1_) | copy-start | bytes 1179652
  60.6 21.6 %all-to-all-start.1 = ((f32[16,3,2,24,128]{4,3,2,1,0:T(8,128)}), f32[16,3,2,24,128]{4,3,2,1,0:T(8,128)S(1)}, u32[]{:S(2)}, u32[]{:S(2)}) async-start(f32[16,3,2,24,128]{4,3,2,1,0:T(8,128)} %shard_map.92), calls=%async_computation.1 | async-start | bytes 2359296 | tf_op jit(solution)/shard_map/all_to_all | solution.py:496
  82.3 12.9 %all-to-all-start.3 = ((f32[16,1,2,24,128]{4,3,2,1,0:T(8,128)}), f32[16,1,2,24,128]{4,3,2,1,0:T(8,128)S(1)}, u32[]{:S(2)}, u32[]{:S(2)}) async-start(f32[16,1,2,24,128]{4,3,2,1,0:T(8,128)} %shard_map.94), calls=%async_computation.3 | async-start | bytes 786432 | tf_op jit(solution)/shard_map/all_to_all | solution.py:496
  91.2 13.4 %copy-start.3 = (f32[864,128]{1,0:T(8,128)S(1)}, f32[864,128]{1,0:T(8,128)}, u32[]{:S(2)}) copy-start(f32[864,128]{1,0:T(8,128)} %get-tuple-element.13) | copy-start | bytes 1327108
  91.2 12.1 %collective-permute-start.4 = (f32[864,128]{1,0:T(8,128)}, f32[864,128]{1,0:T(8,128)S(1)}, u32[]{:S(2)}, u32[]{:S(2)}) collective-permute-start(f32[864,128]{1,0:T(8,128)} %get-tuple-element.17), channel_id=1, source_target_pairs={{0,48},{32,16},{16,64},{48,96},{64,80},{96,112},{80,0},{112,32},{1... | collective-permute-start | bytes 1327112 | tf_op jit(solution)/shard_map/ppermute | solution.py:492
  91.3 13.3 %collective-permute-start.5 = (f32[864,128]{1,0:T(8,128)}, f32[864,128]{1,0:T(8,128)S(1)}, u32[]{:S(2)}, u32[]{:S(2)}) collective-permute-start(f32[864,128]{1,0:T(8,128)} %get-tuple-element.18), channel_id=1, source_target_pairs={{0,112},{32,80},{16,0},{48,32},{64,48},{96,16},{80,96},{112,64},{1... | collective-permute-start | bytes 1327112 | tf_op jit(solution)/shard_map/ppermute | solution.py:492
  98.4 6.2 %collective-permute-start.3 = (f32[864,128]{1,0:T(8,128)}, f32[864,128]{1,0:T(8,128)S(1)}, u32[]{:S(2)}, u32[]{:S(2)}) collective-permute-start(f32[864,128]{1,0:T(8,128)} %get-tuple-element.16), channel_id=1, source_target_pairs={{0,32},{32,0},{16,48},{48,16},{64,96},{96,64},{80,112},{112,80},{1... | collective-permute-start | bytes 1327112 | tf_op jit(solution)/shard_map/ppermute | solution.py:492
where the time goes:
time: 108 us; the launch traced here: 106 us
  waiting for transfers between devices  55.7 us (52%)
  Pallas kernels  25.4 us (24%)
  starting transfers between devices  23.2 us (21%)
  other arithmetic  1.87 us (2%)
    all_to_all x4, waiting for transfers between devices, transpose(): return lax.all_to_all(chunks, 'pencil', 0, 0, tiled=True)  36.8 us
    pallas_call x6, Pallas kernels, call(): pl.pallas_call(entry, out_shape=out_shapes, in_specs=[specs[place] for pl...  25.4 us
    all_to_all x4, starting transfers between devices, transpose(): return lax.all_to_all(chunks, 'pencil', 0, 0, tiled=True)  19 us
    ppermute x3, waiting for transfers between devices, fetch(): return lax.ppermute(block, ('kpair', 'band'), route(kind))  12.9 us
    ppermute x3, waiting for transfers between devices, give_back(): lax.ppermute(block, ('kpair', 'band'), [(b, a) for a, b in route(kind)])  6.06 us
    ppermute x3, starting transfers between devices, fetch(): return lax.ppermute(block, ('kpair', 'band'), route(kind))  2.96 us
  transfers between devices with their start and end apart: 10, of which 9 were waited for; matrix products, arithmetic and copies ran while one was open for 0% of the time, Pallas kernels for 19%

commit v1 on v0

--- a/solution.py
+++ b/solution.py
@@ -292,11 +292,11 @@
     ]
 
 
-def densities(tasks, orbitals, where=place, interpret=False):
+def densities(tasks, orbitals, kept, where=place, interpret=False):
     n = len(tasks)
     (out,) = call(
         lambda *refs: density_kernel(tasks, len(orbitals), where, *refs),
-        [pltpu.HBM((PENCILS * n * 2 * CHUNK, LANES), f32)],
+        [kept((PENCILS * n * 2 * CHUNK, LANES), f32)],
         scratch_fields(),
         [*orbitals, ("hbm", TABLES["forward_z"]), ("hbm", TABLES["forward_y"])],
         interpret,
@@ -304,8 +304,10 @@
     return out.reshape(PENCILS, n, 2, CHUNK, LANES)
 
 
-def filter_kernel(tasks, where, coords, chunks, lanes, forward_table, inverse_table, out_ref):
-    coords_ref, in_ref, lanes_ref = coords.get(), chunks.get(), lanes.get()
+def filter_kernel(groups, where, coords, *refs):
+    chunks, (lanes, forward_table, inverse_table, out_ref) = refs[: len(groups)], refs[len(groups) :]
+    coords_ref, lanes_ref = coords.get(), lanes.get()
+    work = [(kind, chunks[g], i) for g, tasks in enumerate(groups) for i, (kind, _, _) in enumerate(tasks)]
     kpair, band, pencil = where()
     right, left = partners(kpair, band)
     points = {
@@ -323,7 +325,8 @@
     kz = lanes_ref[1:2, :]
     index = lax.broadcasted_iota(jnp.int32, (GRID, 2 * LANES), 0)
     kx = jnp.where(index < GRID // 2, index, index - GRID).astype(f32)
-    for task, (kind, _, _) in enumerate(tasks):
+    for task, (kind, source, place) in enumerate(work):
+        in_ref = source.get()
         here, there = points[kind]
         shift = [(coords_ref[here, a] - coords_ref[there, a]).astype(f32) * 0.25 for a in range(3)]
         plane = (ky + shift[1]) ** 2 + (kz + shift[2]) ** 2
@@ -331,7 +334,7 @@
         previous = None
         for h in range(2):
             rows = [
-                in_ref[:, task, l, 8 * h : 8 * h + 16, :].reshape(256, LANES) for l in range(2)
+                in_ref[:, place, l, 8 * h : 8 * h + 16, :].reshape(256, LANES) for l in range(2)
             ]
             high, low = split(jnp.concatenate(rows, axis=1))
             forward_ref = forward_table.get()
@@ -354,14 +357,15 @@
             previous = back
 
 
-def filtered(tasks, coords, chunks, source, where=place, interpret=False):
+def filtered(groups, coords, chunks, where=place, interpret=False):
+    n = sum(len(tasks) for tasks in groups)
     (out,) = call(
-        lambda *refs: filter_kernel(tasks, where, *refs),
-        [pltpu.HBM(chunks.shape, f32)],
+        lambda *refs: filter_kernel(groups, where, *refs),
+        [jax.ShapeDtypeStruct((PENCILS, n, 2, CHUNK, LANES), f32)],
         [],
         [
             ("smem", coords),
-            (source, chunks),
+            *chunks,
             ("hbm", TABLES["lanes"]),
             ("hbm", TABLES["forward_x"]),
             ("hbm", TABLES["inverse_x"]),
@@ -371,18 +375,18 @@
     return out
 
 
-def potential_kernel(tasks, members, where, chunks, *refs):
-    n = len(tasks)
+def potential_kernel(tasks, first, n, members, bases, where, chunks, *refs):
     in_ref = chunks.get()
-    orbitals = refs[:members]
-    y_table, z_table = refs[members : members + 2]
-    sum_refs = refs[members + 2 : 2 * members + 2]
-    pot_ref, high_ref, low_ref = refs[2 * members + 2 :]
-    touched = set()
+    orbitals, refs = refs[:members], refs[members:]
+    y_table, z_table, refs = refs[0], refs[1], refs[2:]
+    started, refs = refs[:bases], refs[bases:]
+    sum_refs = refs[:members]
+    pot_ref, high_ref, low_ref = refs[members:]
+    earlier = dict(enumerate(started))
     kpair, _, _ = where()
     lane = lane_index(24)
     lane16 = lane_index(16)
-    for task, (kind, a, b) in enumerate(tasks):
+    for task, (kind, a, b) in enumerate(tasks, first):
         for x in range(0, SLAB, 2):
             pair = []
             for v in (x, x + 1):
@@ -438,25 +442,27 @@
             there_real = jnp.where(packed, far_real * pot_imag, there_real)
             there_imag = jnp.where(packed, far_imag * pot_imag, there_imag)
         for member, real, imag in ((a, here_real, here_imag), (b, there_real, there_imag)):
-            if member in touched:
-                real = real + sum_refs[member][0:ROWS, :]
-                imag = imag + sum_refs[member][ROWS : 2 * ROWS, :]
-            touched.add(member)
+            if member in earlier:
+                base_ref = earlier[member].get()
+                real = real + base_ref[0:ROWS, :]
+                imag = imag + base_ref[ROWS : 2 * ROWS, :]
+            earlier[member] = Ready(sum_refs[member])
             sum_refs[member][0:ROWS, :] = real
             sum_refs[member][ROWS : 2 * ROWS, :] = imag
 
 
-def potentials(tasks, chunks, orbitals, where=place, interpret=False):
-    n = len(tasks)
+def potentials(tasks, first, chunks, orbitals, kept, bases=(), where=place, interpret=False):
+    n = chunks.shape[1]
     return call(
-        lambda *refs: potential_kernel(tasks, len(orbitals), where, *refs),
-        [pltpu.HBM((2 * ROWS, LANES), f32)] * len(orbitals),
+        lambda *refs: potential_kernel(tasks, first, n, len(orbitals), len(bases), where, *refs),
+        kept,
         scratch_fields(),
         [
             ("vmem", chunks.reshape(PENCILS * n * 2 * CHUNK, LANES)),
             *orbitals,
             ("hbm", TABLES["inverse_y"]),
             ("hbm", TABLES["inverse_z"]),
+            *bases,
         ],
         interpret,
     )
@@ -496,25 +502,28 @@
     return lax.all_to_all(chunks, "pencil", 0, 0, tiled=True)
 
 
+DENSE = (2 * ROWS, LANES)
+
+
 def body(orbitals, kcoords):
-    own = orbitals.reshape(2 * ROWS, LANES)
+    own = orbitals.reshape(DENSE)
     right, left, other = fetch("right", own), fetch("left", own), fetch("local", own)
     near = [("hbm", own), ("vmem", other)]
     far = [("hbm", own), ("vmem", right), ("vmem", left)]
-    chunks_near = densities(LOCAL, near)
+    chunks_near = densities(LOCAL, near, pltpu.HBM)
     sent_near = transpose(chunks_near)
-    chunks_far = densities(REMOTE, far)
+    chunks_far = densities(REMOTE, far, jax.ShapeDtypeStruct)
     sent_far = transpose(chunks_far)
-    spectrum_near = filtered(LOCAL, kcoords, sent_near, "hbm")
-    spectrum_far = filtered(REMOTE, kcoords, sent_far, "vmem")
-    back_far = transpose(spectrum_far)
-    back_far, spectrum_near = lax.optimization_barrier((back_far, spectrum_near))
-    back_near = transpose(spectrum_near)
-    far_sum, for_right, for_left = potentials(REMOTE, back_far, far)
-    from_right, from_left = give_back("right", for_right), give_back("left", for_left)
-    near_sum, for_other = potentials(LOCAL, back_near, near)
+    spectrum = filtered((REMOTE, LOCAL), kcoords, [("vmem", sent_far), ("vmem", sent_near)])
+    back = transpose(spectrum)
+    kept = [jax.ShapeDtypeStruct(DENSE, f32)] * 3
+    far_sum, for_right, for_left = potentials(REMOTE, 0, back, far, kept)
+    from_right = give_back("right", for_right)
+    from_left = give_back("left", for_left)
+    kept = [jax.ShapeDtypeStruct(DENSE, f32)] * 2
+    own_sum, for_other = potentials(LOCAL, len(REMOTE), back, near, kept, [("vmem", far_sum)])
     from_other = give_back("local", for_other)
-    out = (far_sum + near_sum) + from_other + (from_right + from_left)
+    out = own_sum + from_other + (from_right + from_left)
     return out.reshape(2, 1, 1, SLAB, GRID * GRID)
 
 

time: 108 us -> 96 us (0.89)
  blocking collectives: 0 us -> 44.6 us
  waiting for transfers between devices: 55.7 us -> 16.3 us
  starting transfers between devices: 23.2 us -> 14.7 us
  Pallas kernels: 25.4 us -> 18.6 us
    all_to_all x0 -> x2, blocking collectives: none -> 44.6 us  [transpose(): return lax.all_to_all(chunks, 'pencil', 0, 0, tiled=True)]
    all_to_all x4 -> x1, waiting for transfers between devices: 36.8 us -> 5.57 us  [transpose(): return lax.all_to_all(chunks, 'pencil', 0, 0, tiled=True)]
    ppermute x3, waiting for transfers between devices: 12.9 us -> 0.01 us  [fetch(): return lax.ppermute(block, ('kpair', 'band'), route(kind))]
    all_to_all x4 -> x1, starting transfers between devices: 19 us -> 8.17 us  [transpose(): return lax.all_to_all(chunks, 'pencil', 0, 0, tiled=True)]
    pallas_call x6 -> x5, Pallas kernels: 25.4 us -> 18.6 us  [call(): pl.pallas_call(entry, out_shape=out_shapes, in_specs=[specs[place] for pl...]
    ppermute x3, waiting for transfers between devices: 6.06 us -> 10.7 us  [give_back(): lax.ppermute(block, ('kpair', 'band'), [(b, a) for a, b in route(kind)])]
    ppermute x3, starting transfers between devices: 1.25 us -> 3.14 us  [give_back(): lax.ppermute(block, ('kpair', 'band'), [(b, a) for a, b in route(kind)])]
  transfers between devices with their start and end apart: 10 -> 7, of which waited for: 9 -> 2; matrix products, arithmetic and copies ran while one was open for 0% -> 0% of each run, Pallas kernels for 19% -> 8%
where the time goes in v1:
time: 96 us; the launch traced here: 95.2 us
  blocking collectives  44.6 us (46%)
  Pallas kernels  18.6 us (19%)
  waiting for transfers between devices  16.3 us (17%)
  starting transfers between devices  14.7 us (15%)
    all_to_all x2, blocking collectives, transpose(): return lax.all_to_all(chunks, 'pencil', 0, 0, tiled=True)  44.6 us
    pallas_call x5, Pallas kernels, call(): pl.pallas_call(entry, out_shape=out_shapes, in_specs=[specs[place] for pl...  18.6 us
    ppermute x3, waiting for transfers between devices, give_back(): lax.ppermute(block, ('kpair', 'band'), [(b, a) for a, b in route(kind)])  10.7 us
    all_to_all x1, starting transfers between devices, transpose(): return lax.all_to_all(chunks, 'pencil', 0, 0, tiled=True)  8.17 us
    all_to_all x1, waiting for transfers between devices, transpose(): return lax.all_to_all(chunks, 'pencil', 0, 0, tiled=True)  5.57 us
    ppermute x3, starting transfers between devices, fetch(): return lax.ppermute(block, ('kpair', 'band'), route(kind))  3.35 us
    ppermute x3, starting transfers between devices, give_back(): lax.ppermute(block, ('kpair', 'band'), [(b, a) for a, b in route(kind)])  3.14 us
  transfers between devices with their start and end apart: 7, of which 2 were waited for; matrix products, arithmetic and copies ran while one was open for 0% of the time, Pallas kernels for 8%

profile of v1, /device:TPU:0, one launch (start us, length us, event | category | flops | bytes accessed | tf_op | source)
XLA Modules:
  0.0 95.2 jit_solution(9037102977291111204)
XLA Ops:
  0.0 0.0 collective-permute-start.2
  0.0 1.6 %collective-permute-start.1 = (f32[864,128]{1,0:T(8,128)}, f32[864,128]{1,0:T(8,128)S(1)}, u32[]{:S(2)}, u32[]{:S(2)}) collective-permute-start(f32[864,128]{1,0:T(8,128)} %bitcast.9), channel_id=1, source_target_pairs={{112,0},{80,32},{0,16},{32,48},{48,64},{16,96},{96,80},{64,112},{1... | collective-permute-start | bytes 1327112 | tf_op jit(solution)/shard_map/ppermute | solution.py:494
  1.6 1.7 %collective-permute-start = (f32[864,128]{1,0:T(8,128)}, f32[864,128]{1,0:T(8,128)S(1)}, u32[]{:S(2)}, u32[]{:S(2)}) collective-permute-start(f32[864,128]{1,0:T(8,128)} %bitcast.10), channel_id=1, source_target_pairs={{48,0},{16,32},{64,16},{96,48},{80,64},{112,96},{0,80},{32,112},{4... | collective-permute-start | bytes 1327112 | tf_op jit(solution)/shard_map/ppermute | solution.py:494
  3.4 0.0 collective-permute-done.2.refs_1_.refs_2_
  3.4 3.4 %shard_map.92 = f32[768,128]{1,0:T(8,128)} custom-call(f32[864,128]{1,0:T(8,128)} %bitcast.11, f32[864,128]{1,0:T(8,128)S(1)} %collective-permute-done.2.refs_1_.refs_2_, bf16[2,256,256]{2,1,0:T(8,128)(2,1)} %constant.14.clone.refs_3_.refs_2_, bf16[2,192,192]{2,1,0:T(8,128)(2,1)} %constant.15.clone.refs_4_.refs_3_), custom_call_target="tpu_custom_call" | custom-call | tf_op jit(solution)/shard_map/pallas_call | solution.py:203
  6.8 8.2 %all-to-all-start.1 = ((f32[16,1,2,24,128]{4,3,2,1,0:T(8,128)}), f32[16,1,2,24,128]{4,3,2,1,0:T(8,128)S(1)}, u32[]{:S(2)}, u32[]{:S(2)}) async-start(f32[16,1,2,24,128]{4,3,2,1,0:T(8,128)} %bitcast.15), calls=%async_computation.1 | async-start | bytes 786432 | tf_op jit(solution)/shard_map/all_to_all | solution.py:502
  15.0 0.0 collective-permute-done.1.refs_2_.refs_3_
  15.0 0.0 collective-permute-done.refs_1_.refs_2_
  15.0 4.4 %shard_map.91 = f32[2304,128]{1,0:T(8,128)S(1)} custom-call(f32[864,128]{1,0:T(8,128)} %bitcast.12, f32[864,128]{1,0:T(8,128)S(1)} %collective-permute-done.refs_1_.refs_2_, f32[864,128]{1,0:T(8,128)S(1)} %collective-permute-done.1.refs_2_.refs_3_, bf16[2,256,256]{2,1,0:T(8,128)(2,1)} %constant.14.clone.refs_3_.refs_2_, ...), custom_call_target="tpu_custom_call" | custom-call | tf_op jit(solution)/shard_map/pallas_call | solution.py:203
  19.4 0.0 copy-start
  19.4 5.6 %all-to-all-done.1.refs_2_ = f32[16,1,2,24,128]{4,3,2,1,0:T(8,128)S(1)} async-done(((f32[16,1,2,24,128]{4,3,2,1,0:T(8,128)}), f32[16,1,2,24,128]{4,3,2,1,0:T(8,128)S(1)}, u32[]{:S(2)}, u32[]{:S(2)}) %all-to-all-start.1) | async-done | bytes 393248 | tf_op jit(solution)/shard_map/all_to_all | solution.py:502
  25.0 20.6 %all_to_all.15.refs_1_ = f32[16,3,2,24,128]{4,3,2,1,0:T(8,128)S(1)} all-to-all(f32[16,3,2,24,128]{4,3,2,1,0:T(8,128)S(1)} %bitcast.7), channel_id=1, replica_groups=mesh['kpair'=4,'band'=2,'pencil'=16] {'pencil'}, dimensions={0} | all-to-all | bytes 2359296 | tf_op jit(solution)/shard_map/all_to_all | solution.py:502
  45.5 0.0 copy-done
  45.5 4.0 %shard_map.93 = f32[16,4,2,24,128]{4,3,2,1,0:T(8,128)S(1)} custom-call(s32[4,3]{1,0:T(4,128)S(1)} %copy-done, f32[16,3,2,24,128]{4,3,2,1,0:T(8,128)S(1)} %all_to_all.15.refs_1_, f32[16,1,2,24,128]{4,3,2,1,0:T(8,128)S(1)} %all-to-all-done.1.refs_2_, f32[8,512]{1,0:T(8,128)} %constant.16.clone.refs_3_, bf16[2,2,192,256]{3,2,1,0:T(8,128)(2,1)} %constant.17.clone.refs_4_, ...), custom_call_target="tpu_custom_call" | custom-call | tf_op jit(solution)/shard_map/pallas_call | solution.py:203
  49.5 24.1 %all_to_all.16 = f32[16,4,2,24,128]{4,3,2,1,0:T(8,128)S(1)} all-to-all(f32[16,4,2,24,128]{4,3,2,1,0:T(8,128)S(1)} %shard_map.93), channel_id=1, replica_groups=mesh['kpair'=4,'band'=2,'pencil'=16] {'pencil'}, dimensions={0} | all-to-all | bytes 3145728 | tf_op jit(solution)/shard_map/all_to_all | solution.py:502
  73.6 4.5 %shard_map.94 = (f32[864,128]{1,0:T(8,128)S(1)}, f32[864,128]{1,0:T(8,128)S(1)}, f32[864,128]{1,0:T(8,128)S(1)}) custom-call(f32[3072,128]{1,0:T(8,128)S(1)} %bitcast.5, f32[864,128]{1,0:T(8,128)} %bitcast.13, f32[864,128]{1,0:T(8,128)S(1)} %collective-permute-done.refs_1_.refs_2_, f32[864,128]{1,0:T(8,128)S(1)} %collective-permute-done.1.refs_2_.refs_3_, ...), custom_call_target="tpu_custom_call" | custom-call | tf_op jit(solution)/shard_map/pallas_call | solution.py:203
  78.1 2.4 %shard_map.95 = (f32[864,128]{1,0:T(8,128)S(1)}, f32[864,128]{1,0:T(8,128)S(1)}) custom-call(f32[3072,128]{1,0:T(8,128)S(1)} %bitcast.6, f32[864,128]{1,0:T(8,128)} %bitcast.14, f32[864,128]{1,0:T(8,128)S(1)} %collective-permute-done.2.refs_1_.refs_2_, bf16[2,192,192]{2,1,0:T(8,128)(2,1)} %constant.19.clone.refs_4_.refs_3_, ...), custom_call_target="tpu_custom_call" | custom-call | tf_op jit(solution)/shard_map/pallas_call | solution.py:203
  80.5 0.1 collective-permute-start.3
  80.6 1.1 %collective-permute-start.4 = (f32[864,128]{1,0:T(8,128)S(1)}, f32[864,128]{1,0:T(8,128)S(1)}, u32[]{:S(2)}, u32[]{:S(2)}) collective-permute-start(f32[864,128]{1,0:T(8,128)S(1)} %get-tuple-element.13), channel_id=1, source_target_pairs={{0,48},{32,16},{16,64},{48,96},{64,80},{96,112},{80,0},{112,32},{1... | collective-permute-start | bytes 1327112 | tf_op jit(solution)/shard_map/ppermute | solution.py:498
  81.6 2.0 %collective-permute-start.5 = (f32[864,128]{1,0:T(8,128)S(1)}, f32[864,128]{1,0:T(8,128)S(1)}, u32[]{:S(2)}, u32[]{:S(2)}) collective-permute-start(f32[864,128]{1,0:T(8,128)S(1)} %get-tuple-element.14), channel_id=1, source_target_pairs={{0,112},{32,80},{16,0},{48,32},{64,48},{96,16},{80,96},{112,64},{1... | collective-permute-start | bytes 1327112 | tf_op jit(solution)/shard_map/ppermute | solution.py:498
  83.6 0.0 collective-permute-done.3
  83.6 10.7 %collective-permute-done.4 = f32[864,128]{1,0:T(8,128)S(1)} collective-permute-done((f32[864,128]{1,0:T(8,128)S(1)}, f32[864,128]{1,0:T(8,128)S(1)}, u32[]{:S(2)}, u32[]{:S(2)}) %collective-permute-start.4) | collective-permute-done | bytes 442400 | tf_op jit(solution)/shard_map/ppermute | solution.py:498
  94.4 0.0 collective-permute-done.5
  94.4 0.8 add_add_fusion
Async XLA Ops:
  0.0 3.4 %collective-permute-start.2 = (f32[864,128]{1,0:T(8,128)}, f32[864,128]{1,0:T(8,128)S(1)}, u32[]{:S(2)}, u32[]{:S(2)}) collective-permute-start(f32[864,128]{1,0:T(8,128)} %bitcast.8), channel_id=1, source_target_pairs={{32,0},{0,32},{48,16},{16,48},{96,64},{64,96},{112,80},{80,112},{3... | collective-permute-start | bytes 1327112 | tf_op jit(solution)/shard_map/ppermute | solution.py:494
  0.0 15.0 %collective-permute-start.1 = (f32[864,128]{1,0:T(8,128)}, f32[864,128]{1,0:T(8,128)S(1)}, u32[]{:S(2)}, u32[]{:S(2)}) collective-permute-start(f32[864,128]{1,0:T(8,128)} %bitcast.9), channel_id=1, source_target_pairs={{112,0},{80,32},{0,16},{32,48},{48,64},{16,96},{96,80},{64,112},{1... | collective-permute-start | bytes 1327112 | tf_op jit(solution)/shard_map/ppermute | solution.py:494
  1.6 13.4 %collective-permute-start = (f32[864,128]{1,0:T(8,128)}, f32[864,128]{1,0:T(8,128)S(1)}, u32[]{:S(2)}, u32[]{:S(2)}) collective-permute-start(f32[864,128]{1,0:T(8,128)} %bitcast.10), channel_id=1, source_target_pairs={{48,0},{16,32},{64,16},{96,48},{80,64},{112,96},{0,80},{32,112},{4... | collective-permute-start | bytes 1327112 | tf_op jit(solution)/shard_map/ppermute | solution.py:494
  6.8 18.2 %all-to-all-start.1 = ((f32[16,1,2,24,128]{4,3,2,1,0:T(8,128)}), f32[16,1,2,24,128]{4,3,2,1,0:T(8,128)S(1)}, u32[]{:S(2)}, u32[]{:S(2)}) async-start(f32[16,1,2,24,128]{4,3,2,1,0:T(8,128)} %bitcast.15), calls=%async_computation.1 | async-start | bytes 786432 | tf_op jit(solution)/shard_map/all_to_all | solution.py:502
  19.4 26.1 %copy-start = (s32[4,3]{1,0:T(4,128)S(1)}, s32[4,3]{1,0:T(4,128)}, u32[]{:S(2)}) copy-start(s32[4,3]{1,0:T(4,128)} %refs_0_.1) | copy-start | bytes 148
  80.5 3.2 %collective-permute-start.3 = (f32[864,128]{1,0:T(8,128)S(1)}, f32[864,128]{1,0:T(8,128)S(1)}, u32[]{:S(2)}, u32[]{:S(2)}) collective-permute-start(f32[864,128]{1,0:T(8,128)S(1)} %get-tuple-element.12), channel_id=1, source_target_pairs={{0,32},{32,0},{16,48},{48,16},{64,96},{96,64},{80,112},{112,80},{1... | collective-permute-start | bytes 1327112 | tf_op jit(solution)/shard_map/ppermute | solution.py:498
  80.6 13.8 %collective-permute-start.4 = (f32[864,128]{1,0:T(8,128)S(1)}, f32[864,128]{1,0:T(8,128)S(1)}, u32[]{:S(2)}, u32[]{:S(2)}) collective-permute-start(f32[864,128]{1,0:T(8,128)S(1)} %get-tuple-element.13), channel_id=1, source_target_pairs={{0,48},{32,16},{16,64},{48,96},{64,80},{96,112},{80,0},{112,32},{1... | collective-permute-start | bytes 1327112 | tf_op jit(solution)/shard_map/ppermute | solution.py:498
  81.6 12.7 %collective-permute-start.5 = (f32[864,128]{1,0:T(8,128)S(1)}, f32[864,128]{1,0:T(8,128)S(1)}, u32[]{:S(2)}, u32[]{:S(2)}) collective-permute-start(f32[864,128]{1,0:T(8,128)S(1)} %get-tuple-element.14), channel_id=1, source_target_pairs={{0,112},{32,80},{16,0},{48,32},{64,48},{96,16},{80,96},{112,64},{1... | collective-permute-start | bytes 1327112 | tf_op jit(solution)/shard_map/ppermute | solution.py:498

commit v2 on v1

--- a/solution.py
+++ b/solution.py
@@ -105,8 +105,8 @@
         inverse_z=halves(inverse_z.reshape(2 * LANES, 2 * LANES)),
         forward_y=halves(forward_y),
         inverse_y=halves(inverse_y),
-        forward_x=halves(forward_x.reshape(2, 2 * GRID, 256)),
-        inverse_x=halves(inverse_x.reshape(2, 256, 2 * GRID)),
+        forward_x=halves(forward_x.reshape(2, 2 * GRID, 256)).swapaxes(0, 1),
+        inverse_x=halves(inverse_x.reshape(2, 256, 2 * GRID)).swapaxes(0, 1),
         lanes=lanes,
     )
 
@@ -131,9 +131,18 @@
     return right, left
 
 
-def product3(left_high, left_low, right_high, right_low):
+def data_product(left_high, left_low, table_ref):
+    rows = left_high.shape[0]
     dot = lambda a, b: jnp.dot(a, b, preferred_element_type=f32)
-    return dot(left_high, right_high) + (dot(left_high, right_low) + dot(left_low, right_high))
+    both = dot(jnp.concatenate([left_high, left_low], axis=0), table_ref[0])
+    return both[:rows] + (both[rows:] + dot(left_high, table_ref[1]))
+
+
+def table_product(table, right_high, right_low):
+    rows = table.shape[0] // 2
+    dot = lambda a, b: jnp.dot(a, b, preferred_element_type=f32)
+    both = dot(table, right_high)
+    return both[:rows] + (both[rows:] + dot(table[:rows], right_low))
 
 
 def lane_index(rows):
@@ -198,6 +207,8 @@
                 k += 1
             else:
                 handles.append(Ready(ref))
+        for handle in handles:
+            handle.get()
         kernel(*handles, *outputs, *own_scratch)
 
     return pl.pallas_call(
@@ -217,59 +228,55 @@
 REMOTE = (("across", 1, 2), ("right", 0, 1), ("left", 0, 2))
 
 
+def strided(part, x, s):
+    return pl.ds(part * ROWS + x * 72 + s, 24, stride=3)
+
+
 def density_kernel(tasks, members, where, *refs):
     n = len(tasks)
     orbitals = refs[:members]
-    z_table, y_table, out_ref, dens_ref, high_ref, low_ref = refs[members:]
+    z_table, y_table, out_ref = refs[members:]
     kpair, _, _ = where()
     lane = lane_index(24)
     lane16 = lane_index(16)
     for task, (kind, a, b) in enumerate(tasks):
         own_ref, far_ref = orbitals[a].get(), orbitals[b].get()
-        own_real, own_imag = own_ref[0:ROWS, :], own_ref[ROWS : 2 * ROWS, :]
-        far_real, far_imag = far_ref[0:ROWS, :], far_ref[ROWS : 2 * ROWS, :]
-        real = far_real * own_real + far_imag * own_imag
-        imag = far_real * own_imag - far_imag * own_real
-        if kind == "local":
-            packed = kpair % 2 == 1
-            real = jnp.where(packed, own_real * own_real + own_imag * own_imag, real)
-            imag = jnp.where(packed, far_real * far_real + far_imag * far_imag, imag)
-        dens_ref[0:ROWS, :] = real
-        dens_ref[ROWS : 2 * ROWS, :] = imag
-        for c in range(2):
-            cols = slice(c * LANES, (c + 1) * LANES)
-            for x in range(SLAB):
-                first = c * ROWS + x * 72
-                t0, t1, t2 = (dens_ref[pl.ds(first + s, 24, stride=3), :] for s in range(3))
-                rows = (
-                    t0,
-                    jnp.where(lane < 32, pltpu.roll(t0, 32, 1), pltpu.roll(t1, 32, 1)),
-                    jnp.where(lane < 64, pltpu.roll(t1, 64, 1), pltpu.roll(t2, 64, 1)),
-                    pltpu.roll(t2, 96, 1),
-                )
-                high, low = split(jnp.concatenate(rows, axis=0))
-                high_ref[x * GRID : (x + 1) * GRID, cols] = high
-                low_ref[x * GRID : (x + 1) * GRID, cols] = low
-        z_ref = z_table.get()
-        along_z = product3(high_ref[...], low_ref[...], z_ref[0], z_ref[1])
-        high, low = split(along_z)
-        high_ref[...] = high
-        low_ref[...] = low
-        y_ref = y_table.get()
         for x in range(0, SLAB, 2):
-            def columns(ref):
-                return jnp.concatenate(
-                    [
-                        jnp.concatenate(
-                            [ref[v * GRID : (v + 1) * GRID, 0:LANES], ref[v * GRID : (v + 1) * GRID, LANES:]],
-                            axis=0,
-                        )
-                        for v in (x, x + 1)
-                    ],
-                    axis=1,
-                )
-
-            along_y = product3(y_ref[0], y_ref[1], columns(high_ref), columns(low_ref))
+            planes = []
+            for v in (x, x + 1):
+                tiles = ([], [])
+                for s in range(3):
+                    own_real, own_imag = own_ref[strided(0, v, s), :], own_ref[strided(1, v, s), :]
+                    far_real, far_imag = far_ref[strided(0, v, s), :], far_ref[strided(1, v, s), :]
+                    real = far_real * own_real + far_imag * own_imag
+                    imag = far_real * own_imag - far_imag * own_real
+                    if kind == "local":
+                        packed = kpair % 2 == 1
+                        real = jnp.where(packed, own_real * own_real + own_imag * own_imag, real)
+                        imag = jnp.where(packed, far_real * far_real + far_imag * far_imag, imag)
+                    tiles[0].append(real)
+                    tiles[1].append(imag)
+                parts = []
+                for t0, t1, t2 in tiles:
+                    rows = (
+                        t0,
+                        jnp.where(lane < 32, pltpu.roll(t0, 32, 1), pltpu.roll(t1, 32, 1)),
+                        jnp.where(lane < 64, pltpu.roll(t1, 64, 1), pltpu.roll(t2, 64, 1)),
+                        pltpu.roll(t2, 96, 1),
+                    )
+                    parts.append(jnp.concatenate(rows, axis=0))
+                planes.append(jnp.concatenate(parts, axis=1))
+            along_z = data_product(*split(jnp.concatenate(planes, axis=0)), z_table.get())
+            columns = jnp.concatenate(
+                [
+                    jnp.concatenate(
+                        [along_z[v * GRID : (v + 1) * GRID, c * LANES : (c + 1) * LANES] for c in range(2)], axis=0
+                    )
+                    for v in range(2)
+                ],
+                axis=1,
+            )
+            along_y = table_product(y_table.get()[...].reshape(4 * GRID, 2 * GRID), *split(columns))
             for v in range(2):
                 for c in range(2):
                     bands = [
@@ -284,21 +291,13 @@
                         out_ref[pl.ds(row, 16, stride=n * 2 * CHUNK), :] = value
 
 
-def scratch_fields():
-    return [
-        pltpu.VMEM((2 * ROWS, LANES), f32),
-        pltpu.VMEM((SLAB * GRID, 2 * LANES), bf16),
-        pltpu.VMEM((SLAB * GRID, 2 * LANES), bf16),
-    ]
-
-
-def densities(tasks, orbitals, kept, where=place, interpret=False):
+def densities(tasks, orbitals, kept, early, where=place, interpret=False):
     n = len(tasks)
     (out,) = call(
         lambda *refs: density_kernel(tasks, len(orbitals), where, *refs),
         [kept((PENCILS * n * 2 * CHUNK, LANES), f32)],
-        scratch_fields(),
-        [*orbitals, ("hbm", TABLES["forward_z"]), ("hbm", TABLES["forward_y"])],
+        [],
+        [*orbitals, (early, TABLES["forward_z"]), (early, TABLES["forward_y"])],
         interpret,
     )
     return out.reshape(PENCILS, n, 2, CHUNK, LANES)
@@ -338,7 +337,7 @@
             ]
             high, low = split(jnp.concatenate(rows, axis=1))
             forward_ref = forward_table.get()
-            spectrum = product3(forward_ref[0, h], forward_ref[1, h], high, low)
+            spectrum = table_product(forward_ref[h].reshape(4 * GRID, 256), high, low)
             squared = along_x + plane[:, h * 256 : (h + 1) * 256]
             coulomb = jnp.where(
                 squared <= RADIUS * RADIUS, 4.0 * math.pi / (factor * squared + SCREENING), 0.0
@@ -346,7 +345,7 @@
             spectrum = jnp.concatenate([spectrum[:GRID] * coulomb, spectrum[GRID:] * coulomb], axis=0)
             high, low = split(spectrum)
             inverse_ref = inverse_table.get()
-            back = product3(inverse_ref[0, h], inverse_ref[1, h], high, low).reshape(PENCILS, 16, 2 * LANES)
+            back = table_product(inverse_ref[h].reshape(512, 2 * GRID), high, low).reshape(PENCILS, 16, 2 * LANES)
             for l in range(2):
                 part = back[:, :, l * LANES : (l + 1) * LANES]
                 if h == 0:
@@ -366,9 +365,9 @@
         [
             ("smem", coords),
             *chunks,
-            ("hbm", TABLES["lanes"]),
-            ("hbm", TABLES["forward_x"]),
-            ("hbm", TABLES["inverse_x"]),
+            ("vmem", TABLES["lanes"]),
+            ("vmem", TABLES["forward_x"]),
+            ("vmem", TABLES["inverse_x"]),
         ],
         interpret,
     )
@@ -379,9 +378,7 @@
     in_ref = chunks.get()
     orbitals, refs = refs[:members], refs[members:]
     y_table, z_table, refs = refs[0], refs[1], refs[2:]
-    started, refs = refs[:bases], refs[bases:]
-    sum_refs = refs[:members]
-    pot_ref, high_ref, low_ref = refs[members:]
+    started, sum_refs = refs[:bases], refs[bases:]
     earlier = dict(enumerate(started))
     kpair, _, _ = where()
     lane = lane_index(24)
@@ -405,63 +402,67 @@
                         bands.append(jnp.where(lane16 < ca, head, jnp.where(lane16 < ca + cb, tail, 0.0)))
                     parts += bands
                 pair.append(jnp.concatenate(parts, axis=0))
-            high, low = split(jnp.concatenate(pair, axis=1))
-            y_ref = y_table.get()
-            along_y = product3(y_ref[0], y_ref[1], high, low)
-            high, low = split(along_y)
+            columns = jnp.concatenate(pair, axis=1)
+            along_y = table_product(y_table.get()[...].reshape(4 * GRID, 2 * GRID), *split(columns))
+            planes = jnp.concatenate(
+                [
+                    jnp.concatenate(
+                        [along_y[c * GRID : (c + 1) * GRID, v * LANES : (v + 1) * LANES] for c in range(2)], axis=1
+                    )
+                    for v in range(2)
+                ],
+                axis=0,
+            )
+            along_z = data_product(*split(planes), z_table.get())
+            own_ref, far_ref = orbitals[a].get(), orbitals[b].get()
             for v in range(2):
+                tiles = []
                 for c in range(2):
-                    rows = slice((x + v) * GRID, (x + v + 1) * GRID)
-                    cols = slice(c * LANES, (c + 1) * LANES)
-                    high_ref[rows, cols] = high[c * GRID : (c + 1) * GRID, v * LANES : (v + 1) * LANES]
-                    low_ref[rows, cols] = low[c * GRID : (c + 1) * GRID, v * LANES : (v + 1) * LANES]
-        z_ref = z_table.get()
-        along_z = product3(high_ref[...], low_ref[...], z_ref[0], z_ref[1])
-        for c in range(2):
-            for x in range(SLAB):
-                v0, v1, v2, v3 = (
-                    along_z[x * GRID + 24 * j : x * GRID + 24 * j + 24, c * LANES : (c + 1) * LANES]
-                    for j in range(4)
-                )
-                v1, v2, v3 = pltpu.roll(v1, 96, 1), pltpu.roll(v2, 64, 1), pltpu.roll(v3, 32, 1)
-                rows = (jnp.where(lane < 96, v0, v1), jnp.where(lane < 64, v1, v2), jnp.where(lane < 32, v2, v3))
+                    v0, v1, v2, v3 = (
+                        along_z[v * GRID + 24 * j : v * GRID + 24 * j + 24, c * LANES : (c + 1) * LANES]
+                        for j in range(4)
+                    )
+                    v1, v2, v3 = pltpu.roll(v1, 96, 1), pltpu.roll(v2, 64, 1), pltpu.roll(v3, 32, 1)
+                    tiles.append(
+                        (jnp.where(lane < 96, v0, v1), jnp.where(lane < 64, v1, v2), jnp.where(lane < 32, v2, v3))
+                    )
                 for s in range(3):
-                    pot_ref[pl.ds(c * ROWS + x * 72 + s, 24, stride=3), :] = rows[s]
-        own_ref, far_ref = orbitals[a].get(), orbitals[b].get()
-        own_real, own_imag = own_ref[0:ROWS, :], own_ref[ROWS : 2 * ROWS, :]
-        far_real, far_imag = far_ref[0:ROWS, :], far_ref[ROWS : 2 * ROWS, :]
-        pot_real, pot_imag = pot_ref[0:ROWS, :], pot_ref[ROWS : 2 * ROWS, :]
-        here_real = far_real * pot_real - far_imag * pot_imag
-        here_imag = far_real * pot_imag + far_imag * pot_real
-        there_real = own_real * pot_real + own_imag * pot_imag
-        there_imag = own_imag * pot_real - own_real * pot_imag
-        if kind == "local":
-            packed = kpair % 2 == 1
-            here_real = jnp.where(packed, own_real * pot_real, here_real)
-            here_imag = jnp.where(packed, own_imag * pot_real, here_imag)
-            there_real = jnp.where(packed, far_real * pot_imag, there_real)
-            there_imag = jnp.where(packed, far_imag * pot_imag, there_imag)
-        for member, real, imag in ((a, here_real, here_imag), (b, there_real, there_imag)):
-            if member in earlier:
-                base_ref = earlier[member].get()
-                real = real + base_ref[0:ROWS, :]
-                imag = imag + base_ref[ROWS : 2 * ROWS, :]
+                    at_real, at_imag = strided(0, x + v, s), strided(1, x + v, s)
+                    own_real, own_imag = own_ref[at_real, :], own_ref[at_imag, :]
+                    far_real, far_imag = far_ref[at_real, :], far_ref[at_imag, :]
+                    pot_real, pot_imag = tiles[0][s], tiles[1][s]
+                    here_real = far_real * pot_real - far_imag * pot_imag
+                    here_imag = far_real * pot_imag + far_imag * pot_real
+                    there_real = own_real * pot_real + own_imag * pot_imag
+                    there_imag = own_imag * pot_real - own_real * pot_imag
+                    if kind == "local":
+                        packed = kpair % 2 == 1
+                        here_real = jnp.where(packed, own_real * pot_real, here_real)
+                        here_imag = jnp.where(packed, own_imag * pot_real, here_imag)
+                        there_real = jnp.where(packed, far_real * pot_imag, there_real)
+                        there_imag = jnp.where(packed, far_imag * pot_imag, there_imag)
+                    for member, real, imag in ((a, here_real, here_imag), (b, there_real, there_imag)):
+                        if member in earlier:
+                            base_ref = earlier[member].get()
+                            real = real + base_ref[at_real, :]
+                            imag = imag + base_ref[at_imag, :]
+                        sum_refs[member][at_real, :] = real
+                        sum_refs[member][at_imag, :] = imag
+        for member in (a, b):
             earlier[member] = Ready(sum_refs[member])
-            sum_refs[member][0:ROWS, :] = real
-            sum_refs[member][ROWS : 2 * ROWS, :] = imag
-
-
-def potentials(tasks, first, chunks, orbitals, kept, bases=(), where=place, interpret=False):
+
+
+def potentials(tasks, first, chunks, orbitals, kept, early, bases=(), where=place, interpret=False):
     n = chunks.shape[1]
     return call(
         lambda *refs: potential_kernel(tasks, first, n, len(orbitals), len(bases), where, *refs),
         kept,
-        scratch_fields(),
+        [],
         [
             ("vmem", chunks.reshape(PENCILS * n * 2 * CHUNK, LANES)),
             *orbitals,
-            ("hbm", TABLES["inverse_y"]),
-            ("hbm", TABLES["inverse_z"]),
+            (early, TABLES["inverse_y"]),
+            (early, TABLES["inverse_z"]),
             *bases,
         ],
         interpret,
@@ -509,19 +510,19 @@
     own = orbitals.reshape(DENSE)
     right, left, other = fetch("right", own), fetch("left", own), fetch("local", own)
     near = [("hbm", own), ("vmem", other)]
-    far = [("hbm", own), ("vmem", right), ("vmem", left)]
-    chunks_near = densities(LOCAL, near, pltpu.HBM)
+    far = [("vmem", own), ("vmem", right), ("vmem", left)]
+    chunks_near = densities(LOCAL, near, pltpu.HBM, "hbm")
     sent_near = transpose(chunks_near)
-    chunks_far = densities(REMOTE, far, jax.ShapeDtypeStruct)
+    chunks_far = densities(REMOTE, far, jax.ShapeDtypeStruct, "vmem")
     sent_far = transpose(chunks_far)
     spectrum = filtered((REMOTE, LOCAL), kcoords, [("vmem", sent_far), ("vmem", sent_near)])
     back = transpose(spectrum)
     kept = [jax.ShapeDtypeStruct(DENSE, f32)] * 3
-    far_sum, for_right, for_left = potentials(REMOTE, 0, back, far, kept)
+    far_sum, for_right, for_left = potentials(REMOTE, 0, back, far, kept, "vmem")
     from_right = give_back("right", for_right)
     from_left = give_back("left", for_left)
     kept = [jax.ShapeDtypeStruct(DENSE, f32)] * 2
-    own_sum, for_other = potentials(LOCAL, len(REMOTE), back, near, kept, [("vmem", far_sum)])
+    own_sum, for_other = potentials(LOCAL, len(REMOTE), back, near, kept, "hbm", [("vmem", far_sum)])
     from_other = give_back("local", for_other)
     out = own_sum + from_other + (from_right + from_left)
     return out.reshape(2, 1, 1, SLAB, GRID * GRID)

time: 96 us -> 93 us (0.969)
  Pallas kernels: 18.6 us -> 13.1 us
  waiting for transfers between devices: 16.3 us -> 17.5 us
  local copies, waits for them, and re-layouts: 0.01 us -> 0.99 us
    pallas_call x5, Pallas kernels: 18.6 us -> 13.1 us  [call(): pl.pallas_call(entry, out_shape=out_shapes, in_specs=[specs[place] for pl...]
    all_to_all x1, waiting for transfers between devices: 5.57 us -> 6.76 us  [transpose(): return lax.all_to_all(chunks, 'pencil', 0, 0, tiled=True)]
    unnamed x2 -> x18, local copies, waits for them, and re-layouts: 0.01 us -> 0.99 us
  transfers between devices with their start and end apart: 7 -> 7, of which waited for: 2 -> 2; matrix products, arithmetic and copies ran while one was open for 0% -> 0% of each run, Pallas kernels for 8% -> 6%
where the time goes in v2:
time: 93 us; the launch traced here: 92.2 us
  blocking collectives  45 us (48%)
  waiting for transfers between devices  17.5 us (19%)
  starting transfers between devices  14.7 us (16%)
  Pallas kernels  13.1 us (14%)
  local copies, waits for them, and re-layouts  0.99 us (1%)
    all_to_all x2, blocking collectives, transpose(): return lax.all_to_all(chunks, 'pencil', 0, 0, tiled=True)  45 us
    pallas_call x5, Pallas kernels, call(): pl.pallas_call(entry, out_shape=out_shapes, in_specs=[specs[place] for pl...  13.1 us
    ppermute x3, waiting for transfers between devices, give_back(): lax.ppermute(block, ('kpair', 'band'), [(b, a) for a, b in route(kind)])  10.7 us
    all_to_all x1, starting transfers between devices, transpose(): return lax.all_to_all(chunks, 'pencil', 0, 0, tiled=True)  8.17 us
    all_to_all x1, waiting for transfers between devices, transpose(): return lax.all_to_all(chunks, 'pencil', 0, 0, tiled=True)  6.76 us
    ppermute x3, starting transfers between devices, fetch(): return lax.ppermute(block, ('kpair', 'band'), route(kind))  3.35 us
    ppermute x3, starting transfers between devices, give_back(): lax.ppermute(block, ('kpair', 'band'), [(b, a) for a, b in route(kind)])  3.14 us
  transfers between devices with their start and end apart: 7, of which 2 were waited for; matrix products, arithmetic and copies ran while one was open for 0% of the time, Pallas kernels for 6%

profile of v2, /device:TPU:0, one launch (start us, length us, event | category | flops | bytes accessed | tf_op | source)
XLA Modules:
  0.0 92.2 jit_solution(1495202331187552824)
XLA Ops:
  0.0 1.7 %collective-permute-start.1 = (f32[864,128]{1,0:T(8,128)}, f32[864,128]{1,0:T(8,128)S(1)}, u32[]{:S(2)}, u32[]{:S(2)}) collective-permute-start(f32[864,128]{1,0:T(8,128)} %bitcast.8), channel_id=1, source_target_pairs={{112,0},{80,32},{0,16},{32,48},{48,64},{16,96},{96,80},{64,112},{1... | collective-permute-start | bytes 1327112 | tf_op jit(solution)/shard_map/ppermute | solution.py:495
  1.7 1.7 %collective-permute-start = (f32[864,128]{1,0:T(8,128)}, f32[864,128]{1,0:T(8,128)S(1)}, u32[]{:S(2)}, u32[]{:S(2)}) collective-permute-start(f32[864,128]{1,0:T(8,128)} %bitcast.9), channel_id=1, source_target_pairs={{48,0},{16,32},{64,16},{96,48},{80,64},{112,96},{0,80},{32,112},{4... | collective-permute-start | bytes 1327112 | tf_op jit(solution)/shard_map/ppermute | solution.py:495
  3.4 0.0 collective-permute-done.2.refs_1_.refs_2_
  3.4 3.2 %shard_map.92 = f32[768,128]{1,0:T(8,128)} custom-call(f32[864,128]{1,0:T(8,128)} %bitcast.10, f32[864,128]{1,0:T(8,128)S(1)} %collective-permute-done.2.refs_1_.refs_2_, bf16[2,256,256]{2,1,0:T(8,128)(2,1)} %constant.14.clone.refs_3_.refs_2_, bf16[2,192,192]{2,1,0:T(8,128)(2,1)} %constant.15.clone.refs_4_.refs_3_), custom_call_target="tpu_custom_call" | custom-call | tf_op jit(solution)/shard_map/pallas_call | solution.py:214
  6.6 8.2 %all-to-all-start.1 = ((f32[16,1,2,24,128]{4,3,2,1,0:T(8,128)}), f32[16,1,2,24,128]{4,3,2,1,0:T(8,128)S(1)}, u32[]{:S(2)}, u32[]{:S(2)}) async-start(f32[16,1,2,24,128]{4,3,2,1,0:T(8,128)} %bitcast.15), calls=%async_computation.1 | async-start | bytes 786432 | tf_op jit(solution)/shard_map/all_to_all | solution.py:503
  14.8 0.0 collective-permute-done.1.refs_2_.refs_3_
  14.8 0.0 copy-start.2
  14.8 0.9 %copy-done.2 = bf16[2,256,256]{2,1,0:T(8,128)(2,1)S(1)} copy-done((bf16[2,256,256]{2,1,0:T(8,128)(2,1)S(1)}, bf16[2,256,256]{2,1,0:T(8,128)(2,1)}, u32[]{:S(2)}) %copy-start.2) | copy-done | bytes 262168
  15.8 2.3 %shard_map.91 = f32[2304,128]{1,0:T(8,128)S(1)} custom-call(f32[864,128]{1,0:T(8,128)S(1)} %bitcast.12, f32[864,128]{1,0:T(8,128)S(1)} %collective-permute-done.refs_1_.refs_2_, f32[864,128]{1,0:T(8,128)S(1)} %collective-permute-done.1.refs_2_.refs_3_, bf16[2,256,256]{2,1,0:T(8,128)(2,1)S(1)} %copy-done.2, bf16[2,192,192]{2,1,0:T(8,128)(2,1)S(1)} %copy-done.4), custom_call_target="tpu_custom_call" | custom-call | tf_op jit(solution)/shard_map/pallas_call | solution.py:214
  18.0 0.0 copy-start.7
  18.1 0.0 copy-start.8
  18.1 6.8 %all-to-all-done.1.refs_2_ = f32[16,1,2,24,128]{4,3,2,1,0:T(8,128)S(1)} async-done(((f32[16,1,2,24,128]{4,3,2,1,0:T(8,128)}), f32[16,1,2,24,128]{4,3,2,1,0:T(8,128)S(1)}, u32[]{:S(2)}, u32[]{:S(2)}) %all-to-all-start.1) | async-done | bytes 393248 | tf_op jit(solution)/shard_map/all_to_all | solution.py:503
  24.8 20.8 %all_to_all.15.refs_1_ = f32[16,3,2,24,128]{4,3,2,1,0:T(8,128)S(1)} all-to-all(f32[16,3,2,24,128]{4,3,2,1,0:T(8,128)S(1)} %bitcast.14), channel_id=1, replica_groups=mesh['kpair'=4,'band'=2,'pencil'=16] {'pencil'}, dimensions={0} | all-to-all | bytes 2359296 | tf_op jit(solution)/shard_map/all_to_all | solution.py:503
  45.6 3.0 %shard_map.93 = f32[16,4,2,24,128]{4,3,2,1,0:T(8,128)S(1)} custom-call(s32[4,3]{1,0:T(4,128)S(1)} %copy-done.8, f32[16,3,2,24,128]{4,3,2,1,0:T(8,128)S(1)} %all_to_all.15.refs_1_, f32[16,1,2,24,128]{4,3,2,1,0:T(8,128)S(1)} %all-to-all-done.1.refs_2_, f32[8,512]{1,0:T(8,128)S(1)} %copy-done.7, bf16[2,2,192,256]{3,2,1,0:T(8,128)(2,1)S(1)} %copy-done.6, ...), custom_call_target="tpu_custom_call" | custom-call | tf_op jit(solution)/shard_map/pallas_call | solution.py:214
  48.6 0.0 copy-start.1
  48.6 0.0 copy-start.3
  48.6 24.2 %all_to_all.16 = f32[16,4,2,24,128]{4,3,2,1,0:T(8,128)S(1)} all-to-all(f32[16,4,2,24,128]{4,3,2,1,0:T(8,128)S(1)} %shard_map.93), channel_id=1, replica_groups=mesh['kpair'=4,'band'=2,'pencil'=16] {'pencil'}, dimensions={0} | all-to-all | bytes 3145728 | tf_op jit(solution)/shard_map/all_to_all | solution.py:503
  72.8 2.3 %shard_map.94 = (f32[864,128]{1,0:T(8,128)S(1)}, f32[864,128]{1,0:T(8,128)S(1)}, f32[864,128]{1,0:T(8,128)S(1)}) custom-call(f32[3072,128]{1,0:T(8,128)S(1)} %bitcast.5, f32[864,128]{1,0:T(8,128)S(1)} %bitcast.13, f32[864,128]{1,0:T(8,128)S(1)} %collective-permute-done.refs_1_.refs_2_, f32[864,128]{1,0:T(8,128)S(1)} %collective-permute-done.1.refs_2_.refs_3_, ...), custom_call_target="tpu_custom_call" | custom-call | tf_op jit(solution)/shard_map/pallas_call | solution.py:214
  75.2 2.3 %shard_map.95 = (f32[864,128]{1,0:T(8,128)S(1)}, f32[864,128]{1,0:T(8,128)S(1)}) custom-call(f32[3072,128]{1,0:T(8,128)S(1)} %bitcast.6, f32[864,128]{1,0:T(8,128)} %bitcast.11, f32[864,128]{1,0:T(8,128)S(1)} %collective-permute-done.2.refs_1_.refs_2_, bf16[2,192,192]{2,1,0:T(8,128)(2,1)} %constant.19.clone.refs_4_.refs_3_, ...), custom_call_target="tpu_custom_call" | custom-call | tf_op jit(solution)/shard_map/pallas_call | solution.py:214
  77.5 0.1 collective-permute-start.3
  77.6 1.1 %collective-permute-start.4 = (f32[864,128]{1,0:T(8,128)S(1)}, f32[864,128]{1,0:T(8,128)S(1)}, u32[]{:S(2)}, u32[]{:S(2)}) collective-permute-start(f32[864,128]{1,0:T(8,128)S(1)} %get-tuple-element.13), channel_id=1, source_target_pairs={{0,48},{32,16},{16,64},{48,96},{64,80},{96,112},{80,0},{112,32},{1... | collective-permute-start | bytes 1327112 | tf_op jit(solution)/shard_map/ppermute | solution.py:499
  78.7 1.9 %collective-permute-start.5 = (f32[864,128]{1,0:T(8,128)S(1)}, f32[864,128]{1,0:T(8,128)S(1)}, u32[]{:S(2)}, u32[]{:S(2)}) collective-permute-start(f32[864,128]{1,0:T(8,128)S(1)} %get-tuple-element.14), channel_id=1, source_target_pairs={{0,112},{32,80},{16,0},{48,32},{64,48},{96,16},{80,96},{112,64},{1... | collective-permute-start | bytes 1327112 | tf_op jit(solution)/shard_map/ppermute | solution.py:499
  80.6 10.7 %collective-permute-done.4 = f32[864,128]{1,0:T(8,128)S(1)} collective-permute-done((f32[864,128]{1,0:T(8,128)S(1)}, f32[864,128]{1,0:T(8,128)S(1)}, u32[]{:S(2)}, u32[]{:S(2)}) %collective-permute-start.4) | collective-permute-done | bytes 442400 | tf_op jit(solution)/shard_map/ppermute | solution.py:499
  91.4 0.8 add_add_fusion
  (16 shorter events, 0.0 us)
Async XLA Ops:
  0.0 14.8 %copy-start.4 = (bf16[2,192,192]{2,1,0:T(8,128)(2,1)S(1)}, bf16[2,192,192]{2,1,0:T(8,128)(2,1)}, u32[]{:S(2)}) copy-start(bf16[2,192,192]{2,1,0:T(8,128)(2,1)} %constant.15.clone.refs_4_.refs_3_) | copy-start | bytes 442372
  0.0 14.8 %copy-start = (f32[2,1,1,6,9216]{4,2,3,1,0:T(1,128)S(1)}, f32[2,1,1,6,9216]{4,2,3,1,0:T(1,128)}, u32[]{:S(2)}) copy-start(f32[2,1,1,6,9216]{4,2,3,1,0:T(1,128)} %param.9) | copy-start | bytes 1327108
  0.0 3.4 %collective-permute-start.2 = (f32[864,128]{1,0:T(8,128)}, f32[864,128]{1,0:T(8,128)S(1)}, u32[]{:S(2)}, u32[]{:S(2)}) collective-permute-start(f32[864,128]{1,0:T(8,128)} %bitcast.7), channel_id=1, source_target_pairs={{32,0},{0,32},{48,16},{16,48},{96,64},{64,96},{112,80},{80,112},{3... | collective-permute-start | bytes 1327112 | tf_op jit(solution)/shard_map/ppermute | solution.py:495
  0.0 14.8 %collective-permute-start.1 = (f32[864,128]{1,0:T(8,128)}, f32[864,128]{1,0:T(8,128)S(1)}, u32[]{:S(2)}, u32[]{:S(2)}) collective-permute-start(f32[864,128]{1,0:T(8,128)} %bitcast.8), channel_id=1, source_target_pairs={{112,0},{80,32},{0,16},{32,48},{48,64},{16,96},{96,80},{64,112},{1... | collective-permute-start | bytes 1327112 | tf_op jit(solution)/shard_map/ppermute | solution.py:495
  1.7 13.1 %collective-permute-start = (f32[864,128]{1,0:T(8,128)}, f32[864,128]{1,0:T(8,128)S(1)}, u32[]{:S(2)}, u32[]{:S(2)}) collective-permute-start(f32[864,128]{1,0:T(8,128)} %bitcast.9), channel_id=1, source_target_pairs={{48,0},{16,32},{64,16},{96,48},{80,64},{112,96},{0,80},{32,112},{4... | collective-permute-start | bytes 1327112 | tf_op jit(solution)/shard_map/ppermute | solution.py:495
  6.6 18.2 %all-to-all-start.1 = ((f32[16,1,2,24,128]{4,3,2,1,0:T(8,128)}), f32[16,1,2,24,128]{4,3,2,1,0:T(8,128)S(1)}, u32[]{:S(2)}, u32[]{:S(2)}) async-start(f32[16,1,2,24,128]{4,3,2,1,0:T(8,128)} %bitcast.15), calls=%async_computation.1 | async-start | bytes 786432 | tf_op jit(solution)/shard_map/all_to_all | solution.py:503
  14.8 1.0 %copy-start.2 = (bf16[2,256,256]{2,1,0:T(8,128)(2,1)S(1)}, bf16[2,256,256]{2,1,0:T(8,128)(2,1)}, u32[]{:S(2)}) copy-start(bf16[2,256,256]{2,1,0:T(8,128)(2,1)} %constant.14.clone.refs_3_.refs_2_) | copy-start | bytes 786436
  18.0 27.6 %copy-start.7 = (f32[8,512]{1,0:T(8,128)S(1)}, f32[8,512]{1,0:T(8,128)}, u32[]{:S(2)}) copy-start(f32[8,512]{1,0:T(8,128)} %constant.16.clone.refs_3_) | copy-start | bytes 49156
  18.1 27.5 %copy-start.8 = (s32[4,3]{1,0:T(4,128)S(1)}, s32[4,3]{1,0:T(4,128)}, u32[]{:S(2)}) copy-start(s32[4,3]{1,0:T(4,128)} %refs_0_.1) | copy-start | bytes 148
  24.8 20.8 %copy-start.5 = (bf16[2,2,256,192]{3,2,1,0:T(8,128)(2,1)S(1)}, bf16[2,2,256,192]{3,2,1,0:T(8,128)(2,1)}, u32[]{:S(2)}) copy-start(bf16[2,2,256,192]{3,2,1,0:T(8,128)(2,1)} %constant.18.clone.refs_5_) | copy-start | bytes 1179652
  24.8 20.8 %copy-start.6 = (bf16[2,2,192,256]{3,2,1,0:T(8,128)(2,1)S(1)}, bf16[2,2,192,256]{3,2,1,0:T(8,128)(2,1)}, u32[]{:S(2)}) copy-start(bf16[2,2,192,256]{3,2,1,0:T(8,128)(2,1)} %constant.17.clone.refs_4_) | copy-start | bytes 1179652
  48.6 24.3 %copy-start.1 = (bf16[2,256,256]{2,1,0:T(8,128)(2,1)S(1)}, bf16[2,256,256]{2,1,0:T(8,128)(2,1)}, u32[]{:S(2)}) copy-start(bf16[2,256,256]{2,1,0:T(8,128)(2,1)} %constant.20.clone.refs_5_.refs_4_) | copy-start | bytes 786436
  48.6 24.2 %copy-start.3 = (bf16[2,192,192]{2,1,0:T(8,128)(2,1)S(1)}, bf16[2,192,192]{2,1,0:T(8,128)(2,1)}, u32[]{:S(2)}) copy-start(bf16[2,192,192]{2,1,0:T(8,128)(2,1)} %constant.19.clone.refs_4_.refs_3_) | copy-start | bytes 442372
  77.5 3.2 %collective-permute-start.3 = (f32[864,128]{1,0:T(8,128)S(1)}, f32[864,128]{1,0:T(8,128)S(1)}, u32[]{:S(2)}, u32[]{:S(2)}) collective-permute-start(f32[864,128]{1,0:T(8,128)S(1)} %get-tuple-element.12), channel_id=1, source_target_pairs={{0,32},{32,0},{16,48},{48,16},{64,96},{96,64},{80,112},{112,80},{1... | collective-permute-start | bytes 1327112 | tf_op jit(solution)/shard_map/ppermute | solution.py:499
  77.6 13.8 %collective-permute-start.4 = (f32[864,128]{1,0:T(8,128)S(1)}, f32[864,128]{1,0:T(8,128)S(1)}, u32[]{:S(2)}, u32[]{:S(2)}) collective-permute-start(f32[864,128]{1,0:T(8,128)S(1)} %get-tuple-element.13), channel_id=1, source_target_pairs={{0,48},{32,16},{16,64},{48,96},{64,80},{96,112},{80,0},{112,32},{1... | collective-permute-start | bytes 1327112 | tf_op jit(solution)/shard_map/ppermute | solution.py:499
  78.7 12.6 %collective-permute-start.5 = (f32[864,128]{1,0:T(8,128)S(1)}, f32[864,128]{1,0:T(8,128)S(1)}, u32[]{:S(2)}, u32[]{:S(2)}) collective-permute-start(f32[864,128]{1,0:T(8,128)S(1)} %get-tuple-element.14), channel_id=1, source_target_pairs={{0,112},{32,80},{16,0},{48,32},{64,48},{96,16},{80,96},{112,64},{1... | collective-permute-start | bytes 1327112 | tf_op jit(solution)/shard_map/ppermute | solution.py:499

commit v3 on v2

--- a/solution.py
+++ b/solution.py
@@ -232,11 +232,17 @@
     return pl.ds(part * ROWS + x * 72 + s, 24, stride=3)
 
 
-def density_kernel(tasks, members, where, *refs):
+def density_kernel(tasks, members, where, hold, *refs):
     n = len(tasks)
     orbitals = refs[:members]
-    z_table, y_table, out_ref = refs[members:]
+    z_table, y_table, out_ref, count_ref = refs[members:]
     kpair, _, _ = where()
+    if hold:
+        def step(i, carry):
+            count_ref[0] = i
+            return carry
+
+        lax.fori_loop(0, jnp.where(kpair % 2 == 0, hold, 0), step, 0)
     lane = lane_index(24)
     lane16 = lane_index(16)
     for task, (kind, a, b) in enumerate(tasks):
@@ -291,12 +297,12 @@
                         out_ref[pl.ds(row, 16, stride=n * 2 * CHUNK), :] = value
 
 
-def densities(tasks, orbitals, kept, early, where=place, interpret=False):
+def densities(tasks, orbitals, kept, early, hold=0, where=place, interpret=False):
     n = len(tasks)
     (out,) = call(
-        lambda *refs: density_kernel(tasks, len(orbitals), where, *refs),
+        lambda *refs: density_kernel(tasks, len(orbitals), where, hold, *refs),
         [kept((PENCILS * n * 2 * CHUNK, LANES), f32)],
-        [],
+        [pltpu.SMEM((1,), jnp.int32)],
         [*orbitals, (early, TABLES["forward_z"]), (early, TABLES["forward_y"])],
         interpret,
     )
@@ -504,6 +510,7 @@
 
 
 DENSE = (2 * ROWS, LANES)
+HOLD = 1100
 
 
 def body(orbitals, kcoords):
@@ -511,7 +518,7 @@
     right, left, other = fetch("right", own), fetch("left", own), fetch("local", own)
     near = [("hbm", own), ("vmem", other)]
     far = [("vmem", own), ("vmem", right), ("vmem", left)]
-    chunks_near = densities(LOCAL, near, pltpu.HBM, "hbm")
+    chunks_near = densities(LOCAL, near, pltpu.HBM, "hbm", HOLD)
     sent_near = transpose(chunks_near)
     chunks_far = densities(REMOTE, far, jax.ShapeDtypeStruct, "vmem")
     sent_far = transpose(chunks_far)

time: 93 us -> 87.7 us (0.943)
  blocking collectives: 45 us -> 35.7 us
  Pallas kernels: 13.1 us -> 17.7 us
    all_to_all x2, blocking collectives: 45 us -> 35.7 us  [transpose(): return lax.all_to_all(chunks, 'pencil', 0, 0, tiled=True)]
    pallas_call x5, Pallas kernels: 13.1 us -> 17.7 us  [call(): pl.pallas_call(entry, out_shape=out_shapes, in_specs=[specs[place] for pl...]
  transfers between devices with their start and end apart: 7 -> 7, of which waited for: 2 -> 2; matrix products, arithmetic and copies ran while one was open for 0% -> 0% of each run, Pallas kernels for 6% -> 12%
where the time goes in v3:
time: 87.7 us; the launch traced here: 86.9 us
  blocking collectives  35.7 us (41%)
  Pallas kernels  17.7 us (20%)
  waiting for transfers between devices  16.8 us (19%)
  starting transfers between devices  14.7 us (17%)
  local copies, waits for them, and re-layouts  0.99 us (1%)
    all_to_all x2, blocking collectives, transpose(): return lax.all_to_all(chunks, 'pencil', 0, 0, tiled=True)  35.7 us
    pallas_call x5, Pallas kernels, call(): pl.pallas_call(entry, out_shape=out_shapes, in_specs=[specs[place] for pl...  17.7 us
    ppermute x3, waiting for transfers between devices, give_back(): lax.ppermute(block, ('kpair', 'band'), [(b, a) for a, b in route(kind)])  10.7 us
    all_to_all x1, starting transfers between devices, transpose(): return lax.all_to_all(chunks, 'pencil', 0, 0, tiled=True)  8.17 us
    all_to_all x1, waiting for transfers between devices, transpose(): return lax.all_to_all(chunks, 'pencil', 0, 0, tiled=True)  6.09 us
    ppermute x3, starting transfers between devices, fetch(): return lax.ppermute(block, ('kpair', 'band'), route(kind))  3.35 us
    ppermute x3, starting transfers between devices, give_back(): lax.ppermute(block, ('kpair', 'band'), [(b, a) for a, b in route(kind)])  3.14 us
  transfers between devices with their start and end apart: 7, of which 2 were waited for; matrix products, arithmetic and copies ran while one was open for 0% of the time, Pallas kernels for 12%

profile of v3, /device:TPU:0, one launch (start us, length us, event | category | flops | bytes accessed | tf_op | source)
XLA Modules:
  0.0 86.9 jit_solution(5136473165225324758)
XLA Ops:
  0.0 1.7 %collective-permute-start.1 = (f32[864,128]{1,0:T(8,128)}, f32[864,128]{1,0:T(8,128)S(1)}, u32[]{:S(2)}, u32[]{:S(2)}) collective-permute-start(f32[864,128]{1,0:T(8,128)} %bitcast.8), channel_id=1, source_target_pairs={{112,0},{80,32},{0,16},{32,48},{48,64},{16,96},{96,80},{64,112},{1... | collective-permute-start | bytes 1327112 | tf_op jit(solution)/shard_map/ppermute | solution.py:501
  1.7 1.7 %collective-permute-start = (f32[864,128]{1,0:T(8,128)}, f32[864,128]{1,0:T(8,128)S(1)}, u32[]{:S(2)}, u32[]{:S(2)}) collective-permute-start(f32[864,128]{1,0:T(8,128)} %bitcast.9), channel_id=1, source_target_pairs={{48,0},{16,32},{64,16},{96,48},{80,64},{112,96},{0,80},{32,112},{4... | collective-permute-start | bytes 1327112 | tf_op jit(solution)/shard_map/ppermute | solution.py:501
  3.4 0.0 collective-permute-done.2.refs_1_.refs_2_
  3.4 7.9 %shard_map.92 = f32[768,128]{1,0:T(8,128)} custom-call(f32[864,128]{1,0:T(8,128)} %bitcast.10, f32[864,128]{1,0:T(8,128)S(1)} %collective-permute-done.2.refs_1_.refs_2_, bf16[2,256,256]{2,1,0:T(8,128)(2,1)} %constant.14.clone.refs_3_.refs_2_, bf16[2,192,192]{2,1,0:T(8,128)(2,1)} %constant.15.clone.refs_4_.refs_3_), custom_call_target="tpu_custom_call" | custom-call | tf_op jit(solution)/shard_map/pallas_call | solution.py:214
  11.2 8.2 %all-to-all-start.1 = ((f32[16,1,2,24,128]{4,3,2,1,0:T(8,128)}), f32[16,1,2,24,128]{4,3,2,1,0:T(8,128)S(1)}, u32[]{:S(2)}, u32[]{:S(2)}) async-start(f32[16,1,2,24,128]{4,3,2,1,0:T(8,128)} %bitcast.15), calls=%async_computation.1 | async-start | bytes 786432 | tf_op jit(solution)/shard_map/all_to_all | solution.py:509
  19.5 0.0 copy-start.2
  19.5 0.9 %copy-done.2 = bf16[2,256,256]{2,1,0:T(8,128)(2,1)S(1)} copy-done((bf16[2,256,256]{2,1,0:T(8,128)(2,1)S(1)}, bf16[2,256,256]{2,1,0:T(8,128)(2,1)}, u32[]{:S(2)}) %copy-start.2) | copy-done | bytes 262168
  20.4 2.3 %shard_map.91 = f32[2304,128]{1,0:T(8,128)S(1)} custom-call(f32[864,128]{1,0:T(8,128)S(1)} %bitcast.12, f32[864,128]{1,0:T(8,128)S(1)} %collective-permute-done.refs_1_.refs_2_, f32[864,128]{1,0:T(8,128)S(1)} %collective-permute-done.1.refs_2_.refs_3_, bf16[2,256,256]{2,1,0:T(8,128)(2,1)S(1)} %copy-done.2, bf16[2,192,192]{2,1,0:T(8,128)(2,1)S(1)} %copy-done.4), custom_call_target="tpu_custom_call" | custom-call | tf_op jit(solution)/shard_map/pallas_call | solution.py:214
  22.7 0.0 copy-start.7
  22.7 0.0 copy-start.8
  22.7 6.1 %all-to-all-done.1.refs_2_ = f32[16,1,2,24,128]{4,3,2,1,0:T(8,128)S(1)} async-done(((f32[16,1,2,24,128]{4,3,2,1,0:T(8,128)}), f32[16,1,2,24,128]{4,3,2,1,0:T(8,128)S(1)}, u32[]{:S(2)}, u32[]{:S(2)}) %all-to-all-start.1) | async-done | bytes 393248 | tf_op jit(solution)/shard_map/all_to_all | solution.py:509
  28.8 16.7 %all_to_all.15.refs_1_ = f32[16,3,2,24,128]{4,3,2,1,0:T(8,128)S(1)} all-to-all(f32[16,3,2,24,128]{4,3,2,1,0:T(8,128)S(1)} %bitcast.14), channel_id=1, replica_groups=mesh['kpair'=4,'band'=2,'pencil'=16] {'pencil'}, dimensions={0} | all-to-all | bytes 2359296 | tf_op jit(solution)/shard_map/all_to_all | solution.py:509
  45.6 3.0 %shard_map.93 = f32[16,4,2,24,128]{4,3,2,1,0:T(8,128)S(1)} custom-call(s32[4,3]{1,0:T(4,128)S(1)} %copy-done.8, f32[16,3,2,24,128]{4,3,2,1,0:T(8,128)S(1)} %all_to_all.15.refs_1_, f32[16,1,2,24,128]{4,3,2,1,0:T(8,128)S(1)} %all-to-all-done.1.refs_2_, f32[8,512]{1,0:T(8,128)S(1)} %copy-done.7, bf16[2,2,192,256]{3,2,1,0:T(8,128)(2,1)S(1)} %copy-done.6, ...), custom_call_target="tpu_custom_call" | custom-call | tf_op jit(solution)/shard_map/pallas_call | solution.py:214
  48.5 0.0 copy-start.1
  48.6 0.0 copy-start.3
  48.6 19.0 %all_to_all.16 = f32[16,4,2,24,128]{4,3,2,1,0:T(8,128)S(1)} all-to-all(f32[16,4,2,24,128]{4,3,2,1,0:T(8,128)S(1)} %shard_map.93), channel_id=1, replica_groups=mesh['kpair'=4,'band'=2,'pencil'=16] {'pencil'}, dimensions={0} | all-to-all | bytes 3145728 | tf_op jit(solution)/shard_map/all_to_all | solution.py:509
  67.6 2.3 %shard_map.94 = (f32[864,128]{1,0:T(8,128)S(1)}, f32[864,128]{1,0:T(8,128)S(1)}, f32[864,128]{1,0:T(8,128)S(1)}) custom-call(f32[3072,128]{1,0:T(8,128)S(1)} %bitcast.5, f32[864,128]{1,0:T(8,128)S(1)} %bitcast.13, f32[864,128]{1,0:T(8,128)S(1)} %collective-permute-done.refs_1_.refs_2_, f32[864,128]{1,0:T(8,128)S(1)} %collective-permute-done.1.refs_2_.refs_3_, ...), custom_call_target="tpu_custom_call" | custom-call | tf_op jit(solution)/shard_map/pallas_call | solution.py:214
  69.9 2.3 %shard_map.95 = (f32[864,128]{1,0:T(8,128)S(1)}, f32[864,128]{1,0:T(8,128)S(1)}) custom-call(f32[3072,128]{1,0:T(8,128)S(1)} %bitcast.6, f32[864,128]{1,0:T(8,128)} %bitcast.11, f32[864,128]{1,0:T(8,128)S(1)} %collective-permute-done.2.refs_1_.refs_2_, bf16[2,192,192]{2,1,0:T(8,128)(2,1)} %constant.19.clone.refs_4_.refs_3_, ...), custom_call_target="tpu_custom_call" | custom-call | tf_op jit(solution)/shard_map/pallas_call | solution.py:214
  72.2 0.1 collective-permute-start.3
  72.3 0.5 collective-permute-start.4
  72.8 2.6 %collective-permute-start.5 = (f32[864,128]{1,0:T(8,128)S(1)}, f32[864,128]{1,0:T(8,128)S(1)}, u32[]{:S(2)}, u32[]{:S(2)}) collective-permute-start(f32[864,128]{1,0:T(8,128)S(1)} %get-tuple-element.14), channel_id=1, source_target_pairs={{0,112},{32,80},{16,0},{48,32},{64,48},{96,16},{80,96},{112,64},{1... | collective-permute-start | bytes 1327112 | tf_op jit(solution)/shard_map/ppermute | solution.py:505
  75.4 0.0 collective-permute-done.3
  75.4 10.7 %collective-permute-done.4 = f32[864,128]{1,0:T(8,128)S(1)} collective-permute-done((f32[864,128]{1,0:T(8,128)S(1)}, f32[864,128]{1,0:T(8,128)S(1)}, u32[]{:S(2)}, u32[]{:S(2)}) %collective-permute-start.4) | collective-permute-done | bytes 442400 | tf_op jit(solution)/shard_map/ppermute | solution.py:505
  86.1 0.8 add_add_fusion
  (16 shorter events, 0.0 us)
Async XLA Ops:
  0.0 19.5 %copy-start.4 = (bf16[2,192,192]{2,1,0:T(8,128)(2,1)S(1)}, bf16[2,192,192]{2,1,0:T(8,128)(2,1)}, u32[]{:S(2)}) copy-start(bf16[2,192,192]{2,1,0:T(8,128)(2,1)} %constant.15.clone.refs_4_.refs_3_) | copy-start | bytes 442372
  0.0 19.5 %copy-start = (f32[2,1,1,6,9216]{4,2,3,1,0:T(1,128)S(1)}, f32[2,1,1,6,9216]{4,2,3,1,0:T(1,128)}, u32[]{:S(2)}) copy-start(f32[2,1,1,6,9216]{4,2,3,1,0:T(1,128)} %param.9) | copy-start | bytes 1327108
  0.0 3.4 %collective-permute-start.2 = (f32[864,128]{1,0:T(8,128)}, f32[864,128]{1,0:T(8,128)S(1)}, u32[]{:S(2)}, u32[]{:S(2)}) collective-permute-start(f32[864,128]{1,0:T(8,128)} %bitcast.7), channel_id=1, source_target_pairs={{32,0},{0,32},{48,16},{16,48},{96,64},{64,96},{112,80},{80,112},{3... | collective-permute-start | bytes 1327112 | tf_op jit(solution)/shard_map/ppermute | solution.py:501
  0.0 19.4 %collective-permute-start.1 = (f32[864,128]{1,0:T(8,128)}, f32[864,128]{1,0:T(8,128)S(1)}, u32[]{:S(2)}, u32[]{:S(2)}) collective-permute-start(f32[864,128]{1,0:T(8,128)} %bitcast.8), channel_id=1, source_target_pairs={{112,0},{80,32},{0,16},{32,48},{48,64},{16,96},{96,80},{64,112},{1... | collective-permute-start | bytes 1327112 | tf_op jit(solution)/shard_map/ppermute | solution.py:501
  1.7 17.7 %collective-permute-start = (f32[864,128]{1,0:T(8,128)}, f32[864,128]{1,0:T(8,128)S(1)}, u32[]{:S(2)}, u32[]{:S(2)}) collective-permute-start(f32[864,128]{1,0:T(8,128)} %bitcast.9), channel_id=1, source_target_pairs={{48,0},{16,32},{64,16},{96,48},{80,64},{112,96},{0,80},{32,112},{4... | collective-permute-start | bytes 1327112 | tf_op jit(solution)/shard_map/ppermute | solution.py:501
  11.2 17.6 %all-to-all-start.1 = ((f32[16,1,2,24,128]{4,3,2,1,0:T(8,128)}), f32[16,1,2,24,128]{4,3,2,1,0:T(8,128)S(1)}, u32[]{:S(2)}, u32[]{:S(2)}) async-start(f32[16,1,2,24,128]{4,3,2,1,0:T(8,128)} %bitcast.15), calls=%async_computation.1 | async-start | bytes 786432 | tf_op jit(solution)/shard_map/all_to_all | solution.py:509
  19.5 1.0 %copy-start.2 = (bf16[2,256,256]{2,1,0:T(8,128)(2,1)S(1)}, bf16[2,256,256]{2,1,0:T(8,128)(2,1)}, u32[]{:S(2)}) copy-start(bf16[2,256,256]{2,1,0:T(8,128)(2,1)} %constant.14.clone.refs_3_.refs_2_) | copy-start | bytes 786436
  22.7 22.8 %copy-start.7 = (f32[8,512]{1,0:T(8,128)S(1)}, f32[8,512]{1,0:T(8,128)}, u32[]{:S(2)}) copy-start(f32[8,512]{1,0:T(8,128)} %constant.16.clone.refs_3_) | copy-start | bytes 49156
  22.7 22.8 %copy-start.8 = (s32[4,3]{1,0:T(4,128)S(1)}, s32[4,3]{1,0:T(4,128)}, u32[]{:S(2)}) copy-start(s32[4,3]{1,0:T(4,128)} %refs_0_.1) | copy-start | bytes 148
  28.8 16.7 %copy-start.5 = (bf16[2,2,256,192]{3,2,1,0:T(8,128)(2,1)S(1)}, bf16[2,2,256,192]{3,2,1,0:T(8,128)(2,1)}, u32[]{:S(2)}) copy-start(bf16[2,2,256,192]{3,2,1,0:T(8,128)(2,1)} %constant.18.clone.refs_5_) | copy-start | bytes 1179652
  28.8 16.7 %copy-start.6 = (bf16[2,2,192,256]{3,2,1,0:T(8,128)(2,1)S(1)}, bf16[2,2,192,256]{3,2,1,0:T(8,128)(2,1)}, u32[]{:S(2)}) copy-start(bf16[2,2,192,256]{3,2,1,0:T(8,128)(2,1)} %constant.17.clone.refs_4_) | copy-start | bytes 1179652
  48.5 19.0 %copy-start.1 = (bf16[2,256,256]{2,1,0:T(8,128)(2,1)S(1)}, bf16[2,256,256]{2,1,0:T(8,128)(2,1)}, u32[]{:S(2)}) copy-start(bf16[2,256,256]{2,1,0:T(8,128)(2,1)} %constant.20.clone.refs_5_.refs_4_) | copy-start | bytes 786436
  48.6 19.0 %copy-start.3 = (bf16[2,192,192]{2,1,0:T(8,128)(2,1)S(1)}, bf16[2,192,192]{2,1,0:T(8,128)(2,1)}, u32[]{:S(2)}) copy-start(bf16[2,192,192]{2,1,0:T(8,128)(2,1)} %constant.19.clone.refs_4_.refs_3_) | copy-start | bytes 442372
  72.2 3.2 %collective-permute-start.3 = (f32[864,128]{1,0:T(8,128)S(1)}, f32[864,128]{1,0:T(8,128)S(1)}, u32[]{:S(2)}, u32[]{:S(2)}) collective-permute-start(f32[864,128]{1,0:T(8,128)S(1)} %get-tuple-element.12), channel_id=1, source_target_pairs={{0,32},{32,0},{16,48},{48,16},{64,96},{96,64},{80,112},{112,80},{1... | collective-permute-start | bytes 1327112 | tf_op jit(solution)/shard_map/ppermute | solution.py:505
  72.3 13.8 %collective-permute-start.4 = (f32[864,128]{1,0:T(8,128)S(1)}, f32[864,128]{1,0:T(8,128)S(1)}, u32[]{:S(2)}, u32[]{:S(2)}) collective-permute-start(f32[864,128]{1,0:T(8,128)S(1)} %get-tuple-element.13), channel_id=1, source_target_pairs={{0,48},{32,16},{16,64},{48,96},{64,80},{96,112},{80,0},{112,32},{1... | collective-permute-start | bytes 1327112 | tf_op jit(solution)/shard_map/ppermute | solution.py:505
  72.8 13.3 %collective-permute-start.5 = (f32[864,128]{1,0:T(8,128)S(1)}, f32[864,128]{1,0:T(8,128)S(1)}, u32[]{:S(2)}, u32[]{:S(2)}) collective-permute-start(f32[864,128]{1,0:T(8,128)S(1)} %get-tuple-element.14), channel_id=1, source_target_pairs={{0,112},{32,80},{16,0},{48,32},{64,48},{96,16},{80,96},{112,64},{1... | collective-permute-start | bytes 1327112 | tf_op jit(solution)/shard_map/ppermute | solution.py:505
